TPU v7x, 32 devices: a whole 2x2x4 slice. The times are simulated.
32 devices in a mesh: island: 8 (over y, x, core), fsdp: 4 (over z).
Axes of the slice: x: 2, y: 2, z: 4, core: 2. Of those that a mesh axis runs over, the one named last changes fastest.
Arguments:
- tokens: bfloat16 [8, 1024, 8192], P('island', 'fsdp'), may hold values from -6 to 6
- cotangent: bfloat16 [8, 1024, 1024], P('island', 'fsdp'), may hold values from -0.1875 to 0.1875
- params: float32 [8, 8192, 1024], P('island', 'fsdp'), may hold values from -0.18 to 0.18
- first_moment: bfloat16 [8, 8192, 1024], P('island', 'fsdp'), may hold values from -3 to 3
- second_moment: bfloat16 [8, 8192, 1024], P('island', 'fsdp'), may hold values from 0.25 to 4
- base: float32 [8192, 512], P(('fsdp', 'island')), may hold values from -0.18 to 0.18
- outer_momentum: float32 [8192, 512], P(('fsdp', 'island')), may hold values from -0.06 to 0.06
- head_order: int32 [8], replicated, may hold values from 0 to 7, each once
- step_fragment: int32 [1], replicated, may hold values from 0 to 1
Outputs:
- params_out: float32 [8, 8192, 1024], P('island', 'fsdp')
- first_out: bfloat16 [8, 8192, 1024], P('island', 'fsdp')
- second_out: bfloat16 [8, 8192, 1024], P('island', 'fsdp')
- base_out: float32 [8192, 512], P(('fsdp', 'island'))
- momentum_out: float32 [8192, 512], P(('fsdp', 'island'))
All inputs are finite; a program needn't handle non-finite values.
Results may differ from a plain program's by a relative error of at most 0.012.
Values may be sent and summed in bfloat16 or wider, within the bound.
No kernel may reach another device: no remote copies, remote signals or barrier semaphores. Data moves between devices by JAX's collectives and lax.ppermute only.
A program may use at most 128 MiB of HBM per device.

v0:
```python
import jax
import jax.numpy as jnp
from jax import lax
from jax.sharding import PartitionSpec as P

KVH = 8
HD = 128
SYNC = 4


def outer_update(base, outer_momentum, total, islands):
    delta = base - total / islands
    momentum = 0.9 * outer_momentum + delta
    return (base - 0.7 * (delta + 0.9 * momentum), momentum)


def shards(
    tokens,
    cotangent,
    params,
    first_moment,
    second_moment,
    base,
    outer_momentum,
    head_order,
    step_fragment,
):
    local_tokens = tokens[0]
    weights = params[0]
    rows = weights.shape[0]
    width = weights.shape[1]
    block = local_tokens.shape[0]
    columns = lax.all_to_all(tokens, "fsdp", split_axis=2, concat_axis=1, tiled=True)[0]
    piece = lax.all_gather(cotangent, "fsdp", axis=1, tiled=True)
    blocks = piece.shape[1] // block

    def one_block(index, running):
        grads_part = lax.dynamic_slice_in_dim(piece[0], index * block, block, 0)
        token_part = lax.dynamic_slice_in_dim(columns, index * block, block, 0)
        part = lax.dot_general(
            token_part, grads_part, (((0,), (0,)), ((), ())), preferred_element_type=jnp.float32
        )
        part = lax.optimization_barrier(part.astype(jnp.bfloat16)).astype(jnp.float32)
        return running + part

    grad = lax.fori_loop(0, blocks, one_block, jnp.zeros((rows, width), jnp.float32))
    moment_one = 0.9 * first_moment[0].astype(jnp.float32) + 0.1 * grad
    moment_two = 0.95 * second_moment[0].astype(jnp.float32) + 0.05 * grad * grad
    stepped = weights - 0.01 * (moment_one / (jnp.sqrt(moment_two) + 1e-08) + 0.1 * weights)
    heads = lax.dynamic_slice(head_order, (step_fragment[0] * SYNC,), (SYNC,))
    shaped = stepped.reshape(rows, KVH, HD)
    fragment = jnp.take(shaped, heads, axis=1).reshape(rows, SYNC * HD)
    islands = lax.axis_size("island")
    total = lax.psum_scatter(
        fragment.astype(jnp.bfloat16), "island", scatter_dimension=0, tiled=True
    ).astype(jnp.float32)
    base_next, momentum_next = outer_update(base, outer_momentum, total, islands)
    whole_base = lax.all_gather(
        base_next.astype(jnp.bfloat16), "island", axis=0, tiled=True
    ).astype(base_next.dtype)
    updated = shaped.at[:, heads, :].set(whole_base.reshape(rows, SYNC, HD)).reshape(rows, width)
    return (
        updated[None],
        moment_one.astype(jnp.bfloat16)[None],
        moment_two.astype(jnp.bfloat16)[None],
        base_next,
        momentum_next,
    )


def solution(mesh):
    placed = (
        P("island", "fsdp", None),
        P("island", "fsdp", None),
        P("island", "fsdp", None),
        P("island", "fsdp", None),
        P("island", "fsdp", None),
        P(("fsdp", "island"), None),
        P(("fsdp", "island"), None),
        P(),
        P(),
    )
    return jax.shard_map(
        shards,
        mesh=mesh,
        in_specs=placed,
        out_specs=(
            P("island", "fsdp", None),
            P("island", "fsdp", None),
            P("island", "fsdp", None),
            P(("fsdp", "island"), None),
            P(("fsdp", "island"), None),
        ),
        check_vma=False,
    )
```

profile of v0, /device:TPU:0, one launch (start us, length us, event | category | flops | bytes accessed | tf_op | source)
XLA Modules:
  0.0 422.2 jit_solution(16253507385062909303)
XLA Ops:
  7.2 17.8 %copy.73 = bf16[1,256,8192]{1,0,2:T(2,128)(2,1)} copy(bf16[1,256,8192]{2,1,0:T(8,128)(2,1)} %param.11) | data formatting | bytes 8388608 | tf_op args[0]
  24.9 0.5 broadcast.57
  25.4 43.5 %reduce = bf16[8192,256]{1,0:T(8,128)(2,1)} reduce(bf16[8192,1,256]{2,1,0:T(2,128)(2,1)} %bitcast.56, bf16[]{:T(256)} %broadcast.57), dimensions={1}, to_apply=%bitcast.50.reduce_sub_computation | reduce | bytes 8388610
  69.0 5.1 %reshape.62 = bf16[4,2,262144]{2,1,0:T(2,128)(2,1)} reshape(bf16[8192,256]{1,0:T(8,128)(2,1)} %reduce) | data formatting | bytes 8388608
  74.1 6.3 %all-to-all-start = ((bf16[4,2,262144]{2,1,0:T(2,128)(2,1)}), bf16[4,2,262144]{2,1,0:T(2,128)(2,1)}, u32[]{:S(2)}, u32[]{:S(2)}) async-start(bf16[4,2,262144]{2,1,0:T(2,128)(2,1)} %reshape.62), calls=%async_computation | async-start | bytes 8388608 | tf_op jit(solution)/shard_map/all_to_all | solution.py:33
  80.4 0.0 all-gather.3.cloned.1.call-start
  80.4 0.7 all-gather.3.cloned.1.call-update
  81.1 0.2 reduce-scatter.2.cloned.1.call-start
  82.0 9.3 %copy.71 = f32[1,2048,1024]{1,2,0:T(8,128)} copy(f32[1,2048,1024]{2,1,0:T(8,128)} %param.13) | data formatting | bytes 16777216 | tf_op args[2]
  91.3 0.0 copy-start.2
  91.3 6.6 %copy.72 = bf16[1,2048,1024]{1,2,0:T(8,128)(2,1)} copy(bf16[1,2048,1024]{2,1,0:T(8,128)(2,1)} %param.14) | data formatting | bytes 8388608 | tf_op args[3]
  97.9 6.5 %copy.76 = bf16[1,2048,1024]{1,2,0:T(8,128)(2,1)} copy(bf16[1,2048,1024]{2,1,0:T(8,128)(2,1)} %param.15) | data formatting | bytes 8388608 | tf_op args[4]
  104.4 0.0 copy-done.2
  104.4 0.1 compare_and_fusion
  104.5 0.1 broadcast_bitcast_fusion
  104.6 103.0 %all-to-all-done = bf16[4,2,262144]{2,1,0:T(2,128)(2,1)} async-done(((bf16[4,2,262144]{2,1,0:T(2,128)(2,1)}), bf16[4,2,262144]{2,1,0:T(2,128)(2,1)}, u32[]{:S(2)}, u32[]{:S(2)}) %all-to-all-start) | async-done | bytes 4194336 | tf_op jit(solution)/shard_map/all_to_all | solution.py:33
  207.6 7.4 %reshape.63 = bf16[8192,1,256]{2,1,0:T(2,128)(2,1)} reshape(bf16[4,2,262144]{2,1,0:T(2,128)(2,1)} %all-to-all-done) | data formatting | bytes 8388608
  215.0 6.1 %copy.90 = bf16[1,256,8192]{1,2,0:T(8,128)(2,1)} copy(bf16[1,256,8192]{1,0,2:T(2,128)(2,1)} %bitcast.57) | data formatting | bytes 8388608
  221.1 6.2 %copy.74 = bf16[1,4,256,2048]{3,2,1,0:T(8,128)(2,1)} copy(bf16[1,4,256,2048]{2,3,1,0:T(8,128)(2,1)} %bitcast.60) | data formatting | bytes 8388608 | tf_op jit(solution)/shard_map/all_to_all | solution.py:33
  227.3 0.0 all-gather.3.cloned.1.call-done
  227.3 57.0 %while.14 = (s32[]{:T(128)}, f32[2048,1024]{1,0:T(8,128)}, bf16[1024,2048]{1,0:T(8,128)(2,1)}, bf16[1,1024,1024]{2,1,0:T(8,128)(2,1)}, s32[]{:T(128)}, /*index=5*/s32[]{:T(128)}, s32[]{:T(128)}, s32[]{:T(128)}) while((s32[]{:T(128)}, f32[2048,1024]{1,0:T(8,128)}, bf16[1024,2048]{1,0:T(8,128)(2,1)}, ...), condition=%wide.region_1.0_spmd.clone, body=%wide.region_0.0_spmd.clone.sunk | while | flops 1082130432 | bytes 26739852 | solution.py:46
  227.3 4.7 %convolution_convert_fusion.2 = bf16[2048,1024]{1,0:T(8,128)(2,1)} fusion(bf16[1024,2048]{1,0:T(8,128)(2,1)} %get-tuple-element.179, s32[]{:T(128)S(6)} %select_n.32, bf16[1,1024,1024]{2,1,0:T(8,128)(2,1)} %get-tuple-element.180), kind=kOutput, calls=%fused_computation.3.clone.1 | convolution fusion | flops 1075838976 | bytes 5768192 | tf_op jit(solution)/shard_map/while/body/eval_jaxpr/dot_general | solution.py:40
  231.9 7.8 %select_add_fusion.2 = f32[2048,1024]{1,0:T(8,128)} fusion(f32[2048,1024]{1,0:T(8,128)} %get-tuple-element.170, bf16[2048,1024]{1,0:T(8,128)(2,1)} %convolution_convert_fusion.2, pred[]{:T(512)S(6)} %compare.3), kind=kLoop, calls=%fused_computation.2.clone.1 | loop fusion | flops 6291456 | bytes 20971520 | tf_op jit(solution)/shard_map/while/body/eval_jaxpr/add | solution.py:44
  239.7 4.7 %convolution_convert_fusion.2 = bf16[2048,1024]{1,0:T(8,128)(2,1)} fusion(bf16[1024,2048]{1,0:T(8,128)(2,1)} %get-tuple-element.179, s32[]{:T(128)S(6)} %select_n.32, bf16[1,1024,1024]{2,1,0:T(8,128)(2,1)} %get-tuple-element.180), kind=kOutput, calls=%fused_computation.3.clone.1 | convolution fusion | flops 1075838976 | bytes 5768192 | tf_op jit(solution)/shard_map/while/body/eval_jaxpr/dot_general | solution.py:40
  244.4 10.2 %select_add_fusion.2 = f32[2048,1024]{1,0:T(8,128)} fusion(f32[2048,1024]{1,0:T(8,128)} %get-tuple-element.170, bf16[2048,1024]{1,0:T(8,128)(2,1)} %convolution_convert_fusion.2, pred[]{:T(512)S(6)} %compare.3), kind=kLoop, calls=%fused_computation.2.clone.1 | loop fusion | flops 6291456 | bytes 20971520 | tf_op jit(solution)/shard_map/while/body/eval_jaxpr/add | solution.py:44
  254.6 4.7 %convolution_convert_fusion.2 = bf16[2048,1024]{1,0:T(8,128)(2,1)} fusion(bf16[1024,2048]{1,0:T(8,128)(2,1)} %get-tuple-element.179, s32[]{:T(128)S(6)} %select_n.32, bf16[1,1024,1024]{2,1,0:T(8,128)(2,1)} %get-tuple-element.180), kind=kOutput, calls=%fused_computation.3.clone.1 | convolution fusion | flops 1075838976 | bytes 5768192 | tf_op jit(solution)/shard_map/while/body/eval_jaxpr/dot_general | solution.py:40
  259.3 10.2 %select_add_fusion.2 = f32[2048,1024]{1,0:T(8,128)} fusion(f32[2048,1024]{1,0:T(8,128)} %get-tuple-element.170, bf16[2048,1024]{1,0:T(8,128)(2,1)} %convolution_convert_fusion.2, pred[]{:T(512)S(6)} %compare.3), kind=kLoop, calls=%fused_computation.2.clone.1 | loop fusion | flops 6291456 | bytes 20971520 | tf_op jit(solution)/shard_map/while/body/eval_jaxpr/add | solution.py:44
  269.5 4.7 %convolution_convert_fusion.2 = bf16[2048,1024]{1,0:T(8,128)(2,1)} fusion(bf16[1024,2048]{1,0:T(8,128)(2,1)} %get-tuple-element.179, s32[]{:T(128)S(6)} %select_n.32, bf16[1,1024,1024]{2,1,0:T(8,128)(2,1)} %get-tuple-element.180), kind=kOutput, calls=%fused_computation.3.clone.1 | convolution fusion | flops 1075838976 | bytes 5768192 | tf_op jit(solution)/shard_map/while/body/eval_jaxpr/dot_general | solution.py:40
  274.1 10.2 %select_add_fusion.2 = f32[2048,1024]{1,0:T(8,128)} fusion(f32[2048,1024]{1,0:T(8,128)} %get-tuple-element.170, bf16[2048,1024]{1,0:T(8,128)(2,1)} %convolution_convert_fusion.2, pred[]{:T(512)S(6)} %compare.3), kind=kLoop, calls=%fused_computation.2.clone.1 | loop fusion | flops 6291456 | bytes 20971520 | tf_op jit(solution)/shard_map/while/body/eval_jaxpr/add | solution.py:44
  284.3 9.2 %copy.75 = f32[2048,1024]{0,1:T(8,128)} copy(f32[2048,1024]{1,0:T(8,128)} %get-tuple-element.84) | data formatting | bytes 16777216 | tf_op jit(solution)/shard_map/while | solution.py:46
  293.5 15.2 %fusion.9 = (bf16[1,2048,1024]{1,2,0:T(8,128)(2,1)}, f32[2048,1024]{0,1:T(8,128)}, bf16[1,2048,1024]{1,2,0:T(8,128)(2,1)}) fusion(f32[2048,1024]{0,1:T(8,128)} %copy.75, bf16[1,2048,1024]{1,2,0:T(8,128)(2,1)} %copy.76, bf16[1,2048,1024]{1,2,0:T(8,128)(2,1)} %copy.72, f32[1,2048,1024]{1,2,0:T(8,128)} %copy.71), kind=kLoop, calls=%fused_computation.17 | loop fusion | flops 35651584 | bytes 41943040 | tf_op jit(solution)/shard_map/broadcast_in_dim | solution.py:65
  308.7 0.0 copy-start
  308.7 0.0 copy-start.1
  308.7 4.2 gather_fusion
  313.0 1.8 fusion.11
  314.7 0.0 reduce-scatter.2.cloned.1.call-update
  314.7 0.3 all-gather.5.cloned.1.call-start
  315.0 0.0 copy-done
  315.0 0.2 copy.80
  315.2 0.0 copy-done.1
  315.2 0.2 copy.81
  315.4 39.6 %reduce-scatter.2.cloned.1.call-done = bf16[256,512]{0,1:T(8,128)(2,1)} async-done(((bf16[2048,512]{0,1:T(8,128)(2,1)}), bf16[256,512]{0,1:T(8,128)(2,1)}) %reduce-scatter.2.cloned.1.call-update) | async-done | bytes 262160 | tf_op jit(solution)/shard_map/reduce_scatter | solution.py:54
  355.1 1.8 fusion.12
  356.9 0.0 all-gather.5.cloned.1.call-update
  356.9 9.2 %copy.83 = f32[2048,8,128]{2,0,1:T(8,128)} copy(f32[2048,8,128]{0,2,1:T(8,128)} %bitcast.55) | data formatting | bytes 16777216 | tf_op jit(solution)/shard_map/reshape | solution.py:51
  366.1 6.4 %copy.86 = bf16[1,2048,1024]{2,1,0:T(8,128)(2,1)} copy(bf16[1,2048,1024]{1,2,0:T(8,128)(2,1)} %get-tuple-element.134) | data formatting | bytes 8388608
  372.5 6.3 %copy.87 = bf16[1,2048,1024]{2,1,0:T(8,128)(2,1)} copy(bf16[1,2048,1024]{1,2,0:T(8,128)(2,1)} %get-tuple-element.132) | data formatting | bytes 8388608
  378.8 1.0 copy.88
  379.8 1.0 copy.89
  380.8 4.4 %all-gather.5.cloned.1.call-done = bf16[2048,512]{0,1:T(8,128)(2,1)} async-done(((bf16[256,512]{0,1:T(8,128)(2,1)}), bf16[2048,512]{0,1:T(8,128)(2,1)}) %all-gather.5.cloned.1.call-update) | async-done | bytes 2097168 | tf_op jit(solution)/shard_map/all_gather | solution.py:58
  385.2 4.1 copy.82
  389.3 7.9 %scatter_fusion = f32[2048,8,128]{2,0,1:T(8,128)} fusion(f32[2048,8,128]{2,0,1:T(8,128)} %copy.83, s32[4]{0:T(128)S(1)} %get-tuple-element.131, f32[4,2048,128]{2,1,0:T(8,128)} %bitcast.61), kind=kCustom, calls=%fused_computation.1 | custom fusion | bytes 12582928 | tf_op jit(solution)/shard_map/scatter | solution.py:61
  397.2 9.2 %copy.84 = f32[2048,8,128]{0,2,1:T(8,128)} copy(f32[2048,8,128]{2,0,1:T(8,128)} %scatter_fusion) | data formatting | bytes 16777216 | tf_op jit(solution)/shard_map/scatter | solution.py:61
  406.4 9.2 %copy.85 = f32[1,2048,1024]{2,1,0:T(8,128)} copy(f32[1,2048,1024]{1,2,0:T(8,128)} %bitcast.58) | data formatting | bytes 16777216
  (2 shorter events, 0.0 us)
Async XLA Ops:
  74.1 133.5 %all-to-all-start = ((bf16[4,2,262144]{2,1,0:T(2,128)(2,1)}), bf16[4,2,262144]{2,1,0:T(2,128)(2,1)}, u32[]{:S(2)}, u32[]{:S(2)}) async-start(bf16[4,2,262144]{2,1,0:T(2,128)(2,1)} %reshape.62), calls=%async_computation | async-start | bytes 8388608 | tf_op jit(solution)/shard_map/all_to_all | solution.py:33
  80.4 146.9 %all-gather.3.cloned.1.call-start = ((), (), s32[]{:S(2)}) async-start(), calls=%async_computation.2 | async-start | bytes 2621440 | tf_op jit(solution)/shard_map/all_gather | solution.py:34
  81.1 273.9 %reduce-scatter.2.cloned.1.call-start = ((), (), s32[]{:S(2)}) async-start(), calls=%async_computation.3 | async-start | bytes 2359296 | tf_op jit(solution)/shard_map/reduce_scatter | solution.py:54
  91.3 13.1 %copy-start.2 = (s32[8]{0:T(128)S(1)}, s32[8]{0:T(128)}, u32[]{:S(2)}) copy-start(s32[8]{0:T(128)} %param.18) | copy-start | bytes 100
  308.7 6.3 %copy-start = (f32[256,512]{1,0:T(8,128)S(1)}, f32[256,512]{1,0:T(8,128)}, u32[]{:S(2)}) copy-start(f32[256,512]{1,0:T(8,128)} %param.17) | copy-start | bytes 1572868
  308.7 6.5 %copy-start.1 = (f32[256,512]{1,0:T(8,128)S(1)}, f32[256,512]{1,0:T(8,128)}, u32[]{:S(2)}) copy-start(f32[256,512]{1,0:T(8,128)} %param.16) | copy-start | bytes 1572868
  314.7 70.4 %all-gather.5.cloned.1.call-start = ((), (), s32[]{:S(2)}) async-start(), calls=%async_computation.4 | async-start | bytes 2359296 | tf_op jit(solution)/shard_map/all_gather | solution.py:58
Sparse Core Ops, SparseCore 0:
  82.8 77.2 all-gather.2
  314.9 40.1 reduce-scatter.1
  357.1 28.0 all-gather.4
where the time goes:
time: 425 us; the launch traced here: 422 us
  waiting for transfers between devices  148 us (35%)
  local copies, waits for them, and re-layouts  134 us (32%)
  other arithmetic  101 us (24%)
  matrix products  18.6 us (4%)
  between operations  14.5 us (3%)
  starting transfers between devices  6.83 us (2%)
    all_to_all x1, waiting for transfers between devices, shards(): lax.all_to_all(tokens, 'fsdp', split_axis=2, concat_axis=1, tiled=True)[0]  103 us
    unnamed x21, local copies, waits for them, and re-layouts  83.5 us
    unnamed x2, other arithmetic  43.5 us
    reduce_scatter x1, waiting for transfers between devices, shards(): lax.psum_scatter(fragment.astype(jnp.bfloat16), 'island', scatter_dimensi...  39.6 us
    add x4, other arithmetic, one_block(): return running + part  38.4 us
    dot_general x4, matrix products, one_block(): lax.dot_general(token_part, grads_part, (((0,), (0,)), ((), ())), preferr...  18.6 us
    scatter x2, local copies, waits for them, and re-layouts, shards(): shaped.at[:, heads, :].set(whole_base.reshape(rows, SYNC, HD))  17.1 us
    broadcast_in_dim x1, other arithmetic, shards(): moment_two.astype(jnp.bfloat16)[None]  15.2 us
  transfers between devices with their start and end apart: 4, of which 3 were waited for; matrix products, arithmetic and copies ran while one was open for 16% of the time, Pallas kernels for 0%

commit v1 on v0

--- a/solution.py
+++ b/solution.py
@@ -1,7 +1,12 @@
+import functools
+
 import jax
 import jax.numpy as jnp
 from jax import lax
+from jax.experimental import pallas as pl
+from jax.experimental.pallas import tpu as pltpu
 from jax.sharding import PartitionSpec as P
+
 
 KVH = 8
 HD = 128
@@ -14,7 +19,396 @@
     return (base - 0.7 * (delta + 0.9 * momentum), momentum)
 
 
-def shards(
+ANY = pl.BlockSpec(memory_space=pl.ANY)
+HBM = pl.BlockSpec(memory_space=pltpu.HBM)
+
+
+def cost(flops, moved):
+    return pl.CostEstimate(flops=flops, bytes_accessed=moved, transcendentals=0)
+
+
+def head_at(heads_ref, step_ref, position):
+    return heads_ref[lax.rem(step_ref[0] * SYNC + position, KVH)]
+
+
+def column(heads_ref, step_ref, position):
+    return pl.ds(pl.multiple_of(head_at(heads_ref, step_ref, position) * HD, HD), HD)
+
+
+VMEM_GRANT = 67043328 - 56 * 2**18
+
+
+def call(
+    kernel, scalars, args, outs, scratch, estimate, in_specs=None, out_specs=None, aliases=None
+):
+    return pl.pallas_call(
+        kernel,
+        grid_spec=pltpu.PrefetchScalarGridSpec(
+            num_scalar_prefetch=len(scalars),
+            grid=(1,),
+            in_specs=in_specs or [ANY] * len(args),
+            out_specs=out_specs or [ANY] * len(outs),
+            scratch_shapes=scratch,
+        ),
+        out_shape=outs,
+        input_output_aliases=aliases or {},
+        cost_estimate=estimate,
+        compiler_params=pltpu.CompilerParams(vmem_limit_bytes=VMEM_GRANT),
+    )(*scalars, *args)
+
+
+def turn_tokens(table, tokens, owners, peers, span, lanes, cuts):
+    depth = tokens.shape[0]
+    first, count = lanes
+
+    def kernel(table_ref, tok_ref, *refs):
+        outs = refs[: len(cuts) * peers]
+        raw, in_sems, out_sems = refs[len(cuts) * peers : len(cuts) * peers + 3]
+        stages = refs[len(cuts) * peers + 3 :]
+        sequence = [*range(1, peers), 0]
+
+        def load(e, i):
+            start = (table_ref[owners + e] * owners + i) * span + first
+            return pltpu.make_async_copy(
+                tok_ref.at[:, pl.ds(pl.multiple_of(start, HD), count)],
+                raw.at[e, i],
+                in_sems.at[e, i],
+            )
+
+        for e in sequence:
+            for i in range(owners):
+                load(e, i).start()
+        stores = []
+        for e in sequence:
+            for i in range(owners):
+                load(e, i).wait()
+                turned = raw[e, i].T
+                for c, (start, width) in enumerate(cuts):
+                    stages[c][e, i] = turned[start - first : start - first + width]
+            for c in range(len(cuts)):
+                stores.append(
+                    pltpu.make_async_copy(
+                        stages[c].at[e], outs[c * peers + e], out_sems.at[c, e]
+                    )
+                )
+                stores[-1].start()
+        for store in stores:
+            store.wait()
+
+    flat = call(
+        kernel,
+        (table,),
+        (tokens,),
+        [
+            jax.ShapeDtypeStruct((owners, w, depth), tokens.dtype)
+            for _, w in cuts
+            for _ in range(peers)
+        ],
+        [
+            pltpu.VMEM((peers, owners, depth, count), tokens.dtype),
+            pltpu.SemaphoreType.DMA((peers, owners)),
+            pltpu.SemaphoreType.DMA((len(cuts), peers)),
+            *[pltpu.VMEM((peers, owners, w, depth), tokens.dtype) for _, w in cuts],
+        ],
+        cost(0, 4 * peers * owners * count * depth),
+        in_specs=[HBM],
+    )
+    return [flat[c * peers : (c + 1) * peers] for c in range(len(cuts))]
+
+
+def inner_step(heads, step, table, toks, cots, state, olds, place, k0):
+    owners, _, _ = state[0].shape
+    w, depth = toks[0].shape[1:]
+    peers = len(toks)
+    p0, count = place
+    rows = owners * w
+    shared = max(0, min(SYNC - p0, count))
+
+    def kernel(heads_ref, step_ref, table_ref, *refs):
+        tok_refs, refs = refs[:peers], refs[peers:]
+        cot_refs, refs = refs[: len(cots)], refs[len(cots) :]
+        sources, refs = refs[:3], refs[3:]
+        if olds is not None:
+            refs = refs[3:]
+        targets, refs = refs[:3], refs[3:]
+        if shared:
+            keep_ref, send_ref, *refs = refs
+        left, right, grad, p_s, m_s, v_s, tok_sems, cot_sems, in_sems, out_sems = refs
+        parts = (p_s, m_s, v_s)
+        me = table_ref[owners]
+        isle = table_ref[0]
+        inner = (me > 0) & (me < peers - 1)
+
+        def tok_copy(e):
+            return pltpu.make_async_copy(
+                tok_refs[e], left.at[:, :, pl.ds(e * depth, depth)], tok_sems.at[e]
+            )
+
+        def cot_copy(e, k, j):
+            return pltpu.make_async_copy(
+                cot_refs[k].at[:, column(heads_ref, step_ref, p0 + j)],
+                right.at[pl.ds(e * depth, depth), pl.ds(j * HD, HD)],
+                cot_sems.at[e, j],
+            )
+
+        def window(ref, j):
+            return ref.at[:, pl.ds(k0, w), column(heads_ref, step_ref, p0 + j)]
+
+        def in_copy(n, j):
+            return pltpu.make_async_copy(window(sources[n], j), parts[n].at[j], in_sems.at[n, j])
+
+        def out_copy(n, j):
+            return pltpu.make_async_copy(parts[n].at[j], window(targets[n], j), out_sems.at[n, j])
+
+        for e in range(peers):
+            tok_copy(e).start()
+        for j in range(count):
+            for e in range(2):
+                cot_copy(e, e, j).start()
+        for e in range(2, peers):
+
+            @pl.when(inner)
+            def _():
+                for j in range(count):
+                    cot_copy(e, 2 * e - 2, j).start()
+
+            @pl.when(jnp.logical_not(inner))
+            def _():
+                for j in range(count):
+                    cot_copy(e, 2 * e - 1, j).start()
+
+        for j in range(count):
+            for n in range(3):
+                in_copy(n, j).start()
+        for e in range(peers):
+            tok_copy(e).wait()
+            for j in range(count):
+                cot_copy(e, e, j).wait()
+
+        def update(j, lane, owner, target, slot):
+            g = grad[owner, :, lane * HD : (lane + 1) * HD]
+            one = 0.9 * m_s[j, owner].astype(jnp.float32) + 0.1 * g
+            two = 0.95 * v_s[j, owner].astype(jnp.float32) + 0.05 * g * g
+            old = p_s[j, owner]
+            new = old - 0.01 * (one / (jnp.sqrt(two) + 1e-08) + 0.1 * old)
+            m_s[j, owner] = one.astype(m_s.dtype)
+            v_s[j, owner] = two.astype(v_s.dtype)
+            p_s[j, owner] = new
+            if target is not None:
+                lanes = pl.ds(pl.multiple_of(j * HD, HD), HD)
+                target[slot, :, lanes] = new.astype(target.dtype)
+
+        def one_pair(share, pair, carry):
+            lanes = pl.ds(pl.multiple_of(pair * 2 * HD, 2 * HD), 2 * HD)
+            grad[...] = jnp.dot(
+                left[...].reshape(rows, peers * depth),
+                right[:, lanes],
+                preferred_element_type=jnp.float32,
+            ).reshape(owners, w, 2 * HD)
+            for lane in range(2):
+                j = 2 * pair + lane
+                for n in range(3):
+                    in_copy(n, j).wait()
+
+                def two_owners(slot, carry):
+                    for odd, target in enumerate((keep_ref, send_ref) if share else (None, None)):
+                        update(j, lane, (2 * slot + odd) ^ isle, target, slot)
+                    return carry
+
+                lax.fori_loop(0, owners // 2, two_owners, 0)
+                for n in range(3):
+                    out_copy(n, j).start()
+            return carry
+
+        if shared:
+            lax.fori_loop(0, shared // 2, functools.partial(one_pair, True), 0)
+        if shared < count:
+            lax.fori_loop(shared // 2, count // 2, functools.partial(one_pair, False), 0)
+        for j in range(count):
+            for n in range(3):
+                out_copy(n, j).wait()
+
+    args = [*toks, *cots, *state]
+    aliases = {}
+    if olds is not None:
+        for i in range(3):
+            aliases[3 + len(args) + i] = i
+        args += list(olds)
+    outs = [jax.ShapeDtypeStruct(a.shape, a.dtype) for a in state]
+    out_specs = [HBM] * 3
+    if shared:
+        piece = (owners // 2, w, shared * HD)
+        outs += [jax.ShapeDtypeStruct(piece, jnp.bfloat16)] * 2
+        out_specs += [pl.BlockSpec(piece, lambda i, *_: (0, 0, 0))] * 2
+    states = [HBM] * (6 if olds is not None else 3)
+    result = call(
+        kernel,
+        (heads, step, table),
+        args,
+        outs,
+        [
+            pltpu.VMEM((owners, w, peers * depth), toks[0].dtype),
+            pltpu.VMEM((peers * depth, count * HD), cots[0].dtype),
+            pltpu.VMEM((owners, w, 2 * HD), jnp.float32),
+            *[pltpu.VMEM((count, owners, w, HD), a.dtype) for a in state],
+            pltpu.SemaphoreType.DMA((peers,)),
+            pltpu.SemaphoreType.DMA((peers, count)),
+            pltpu.SemaphoreType.DMA((3, count)),
+            pltpu.SemaphoreType.DMA((3, count)),
+        ],
+        cost(
+            2 * rows * depth * peers * count * HD,
+            rows * count * HD * 16 + 2 * rows * depth * peers,
+        ),
+        in_specs=[ANY] * (len(toks) + len(cots)) + states,
+        out_specs=out_specs,
+        aliases=aliases,
+    )
+    return result[:3], result[3:]
+
+
+def place_base(heads, step, table, news, params, starts):
+    owners = params.shape[0]
+    shapes = [near.shape for near, _ in news]
+    count = shapes[0][2] // HD
+
+    def kernel(heads_ref, step_ref, table_ref, *refs):
+        pieces, refs = refs[: 2 * len(news)], refs[2 * len(news) + 1 :]
+        out_ref, stages, sems = refs[0], refs[1:-1], refs[-1]
+        isle = table_ref[0]
+        copies = []
+        for c, (k0, shape) in enumerate(zip(starts, shapes)):
+            for j in range(count):
+                for e in range(owners):
+                    source = pieces[2 * c + e % 2][e // 2, :, j * HD : (j + 1) * HD]
+                    stages[c][j, e ^ isle] = source.astype(jnp.float32)
+                target = out_ref.at[:, pl.ds(k0, shape[1]), column(heads_ref, step_ref, j)]
+                copies.append(pltpu.make_async_copy(stages[c].at[j], target, sems.at[c, j]))
+                copies[-1].start()
+        for copy in copies:
+            copy.wait()
+
+    (out,) = call(
+        kernel,
+        (heads, step, table),
+        (*[x for pair in news for x in pair], params),
+        [jax.ShapeDtypeStruct(params.shape, params.dtype)],
+        [
+            *[pltpu.VMEM((count, owners, shape[1], HD), jnp.float32) for shape in shapes],
+            pltpu.SemaphoreType.DMA((len(news), count)),
+        ],
+        cost(0, sum(owners * shape[1] * shape[2] * 8 for shape in shapes)),
+        in_specs=[
+            pl.BlockSpec(shape, lambda i, *_: (0, 0, 0)) for shape in shapes for _ in range(2)
+        ]
+        + [HBM],
+        out_specs=[HBM],
+        aliases={3 + 2 * len(news): 0},
+    )
+    return out
+
+
+def swap(x, axis, mask):
+    return lax.ppermute(x, axis, [(i, i ^ mask) for i in range(lax.axis_size(axis))])
+
+
+def line_gather(own):
+    middle, ends = [(1, 2), (2, 1)], [(1, 0), (2, 3)]
+    near = swap(own, "fsdp", 1)
+    far = lax.ppermute(own, "fsdp", middle)
+    next_far = lax.ppermute(near, "fsdp", middle)
+    relay = lax.ppermute(far, "fsdp", ends)
+    next_relay = lax.ppermute(next_far, "fsdp", ends)
+    return [own, near, next_far, relay, far, next_relay]
+
+
+def island_sum(keep, give):
+    got = swap(give, "island", 1)
+    part = keep.astype(jnp.float32) + got.astype(jnp.float32)
+    total = part[0]
+    for d in range(1, part.shape[0]):
+        piece = part[d].astype(jnp.bfloat16)
+        total = total + swap(piece, "island", 2 * d).astype(jnp.float32)
+    return total
+
+
+def island_spread(own):
+    chips = lax.axis_size("island") // 2
+    pieces = [own] + [swap(own, "island", 2 * d) for d in range(1, chips)]
+    near = jnp.stack(pieces)
+    return near, swap(near, "island", 1)
+
+
+PLAN = ((0, 9), (9, 4), (13, 3))
+PARTS = 16
+
+
+def staged(
+    tokens,
+    cotangent,
+    params,
+    first_moment,
+    second_moment,
+    base,
+    outer_momentum,
+    head_order,
+    step_fragment,
+):
+    islands = lax.axis_size("island")
+    peers = lax.axis_size("fsdp")
+    rows, width = params.shape[1:]
+    span = rows // islands
+    me = lax.axis_index("fsdp").astype(jnp.int32)
+    isle = lax.axis_index("island").astype(jnp.int32)
+    slots = jnp.arange(islands + peers, dtype=jnp.int32)
+    table = jnp.where(slots < islands, slots ^ isle, (slots - islands) ^ me)
+    hs = (head_order, step_fragment)
+
+    cots = line_gather(cotangent[0])
+    plan = [(k * span // PARTS, n * span // PARTS) for k, n in PLAN]
+    last = len(plan) - 1
+    edge = -(-plan[0][1] // HD) * HD
+    turned = turn_tokens(table, tokens[0], islands, peers, span, (0, edge), plan[:1])
+    edge = plan[1][0] // HD * HD
+    turned += turn_tokens(
+        table, tokens[0], islands, peers, span, (edge, span - edge), plan[1:]
+    )
+    toks = [
+        [pieces[0]] + [swap(pieces[e], "fsdp", e) for e in range(1, peers)]
+        for pieces in turned
+    ]
+
+    state = [a[0].reshape(islands, span, width) for a in (params, first_moment, second_moment)]
+    olds = None
+    bases, momenta, news = [], [], []
+
+    def run(c, place):
+        return inner_step(*hs, table, toks[c], cots, state, olds, place, plan[c][0])
+
+    for c, (k0, w) in enumerate(plan):
+        if c < last:
+            olds, pieces = run(c, (0, KVH))
+        else:
+            olds, pieces = run(c, (0, SYNC))
+            olds, _ = run(c, (SYNC, KVH - SYNC))
+        total = island_sum(*pieces)
+        new, mom = outer_update(base[k0 : k0 + w], outer_momentum[k0 : k0 + w], total, islands)
+        bases.append(new)
+        momenta.append(mom)
+        news.append(island_spread(new.astype(jnp.bfloat16)))
+    starts = [k0 for k0, _ in plan]
+    out = place_base(*hs, table, news[:last], olds[0], starts[:last])
+    out = place_base(*hs, table, news[last:], out, starts[last:])
+    return (
+        out.reshape(1, rows, width),
+        olds[1].reshape(1, rows, width),
+        olds[2].reshape(1, rows, width),
+        jnp.concatenate(bases),
+        jnp.concatenate(momenta),
+    )
+
+
+def plain(
     tokens,
     cotangent,
     params,
@@ -68,6 +462,23 @@
     )
 
 
+def fits(tokens, params, islands, peers):
+    span = params.shape[1] // islands
+    return (
+        peers == 4
+        and islands >= 4
+        and islands & (islands - 1) == 0
+        and span % (2 * HD) == 0
+        and tokens.shape[1] % HD == 0
+    )
+
+
+def shards(tokens, cotangent, params, *rest):
+    sizes = lax.axis_size("island"), lax.axis_size("fsdp")
+    step = staged if fits(tokens, params, *sizes) else plain
+    return step(tokens, cotangent, params, *rest)
+
+
 def solution(mesh):
     placed = (
         P("island", "fsdp", None),

time: 425 us -> 178 us (0.42)
  local copies, waits for them, and re-layouts: 134 us -> 0.95 us
  other arithmetic: 101 us -> 1.98 us
  waiting for transfers between devices: 148 us -> 72 us
  starting transfers between devices: 6.83 us -> 57.2 us
  Pallas kernels: 0 us -> 43.8 us
  matrix products: 18.6 us -> 0 us
  between operations: 14.5 us -> 1.88 us
    all_to_all x1 -> x0, waiting for transfers between devices: 103 us -> none  [shards(): lax.all_to_all(tokens, 'fsdp', split_axis=2, concat_axis=1, tiled=True)[0]]
    unnamed x21 -> x26, local copies, waits for them, and re-layouts: 83.5 us -> 0.89 us
    ppermute x0 -> x38, waiting for transfers between devices: none -> 72 us  [the longest x34 72 us: swap(): lax.ppermute(x, axis, [(i, i ^ mask) for i in range(lax.axis_size(axis))])]
    ppermute x0 -> x38, starting transfers between devices: none -> 57.2 us  [the longest x34 53.3 us: swap(): lax.ppermute(x, axis, [(i, i ^ mask) for i in range(lax.axis_size(axis))])]
    pallas_call x0 -> x8, Pallas kernels: none -> 43.8 us  [call(): pl.pallas_call(kernel, grid_spec=pltpu.PrefetchScalarGridSpec(num_scalar_...]
    unnamed x2 -> x0, other arithmetic: 43.5 us -> none
    reduce_scatter x1 -> x0, waiting for transfers between devices: 39.6 us -> none  [shards(): lax.psum_scatter(fragment.astype(jnp.bfloat16), 'island', scatter_dimensi...]
    add x4 -> x6, other arithmetic: 38.4 us -> 0.61 us  [the longest x3 0.36 us: island_sum(): part = keep.astype(jnp.float32) + got.astype(jnp.float32)]
  transfers between devices with their start and end apart: 4 -> 38, of which waited for: 3 -> 14; matrix products, arithmetic and copies ran while one was open for 16% -> 1% of each run, Pallas kernels for 0% -> 21%
where the time goes in v1:
time: 178 us
  waiting for transfers between devices  72 us (40%)
  starting transfers between devices  57.2 us (32%)
  Pallas kernels  43.8 us (25%)
  other arithmetic  1.98 us (1%)
  between operations  1.88 us (1%)
    ppermute x34, waiting for transfers between devices, swap(): lax.ppermute(x, axis, [(i, i ^ mask) for i in range(lax.axis_size(axis))])  72 us
    ppermute x34, starting transfers between devices, swap(): lax.ppermute(x, axis, [(i, i ^ mask) for i in range(lax.axis_size(axis))])  53.3 us
    pallas_call x8, Pallas kernels, call(): pl.pallas_call(kernel, grid_spec=pltpu.PrefetchScalarGridSpec(num_scalar_...  43.8 us
  transfers between devices with their start and end apart: 38, of which 14 were waited for; matrix products, arithmetic and copies ran while one was open for 1% of the time, Pallas kernels for 21%

profile of v1, /device:TPU:0, one launch (start us, length us, event | category | flops | bytes accessed | tf_op | source)
XLA Modules:
  0.0 177.9 jit_solution(8978130771122297308)
XLA Ops:
  0.6 3.1 %collective-permute-start.3 = (bf16[256,1024]{1,0:T(8,128)(2,1)}, bf16[256,1024]{1,0:T(8,128)(2,1)S(1)}, u32[]{:S(2)}, u32[]{:S(2)}) collective-permute-start(bf16[256,1024]{1,0:T(8,128)(2,1)} %bitcast.77), channel_id=1, source_target_pairs={{0,1},{1,0},{2,3},{3,2},{4,5},{5,4},{6,7},{7,6},{8,9},{9,8},{10,11... | collective-permute-start | bytes 1572872 | tf_op jit(solution)/shard_map/ppermute | solution.py:312
  3.7 0.7 collective-permute-start.5
  4.4 11.4 %collective-permute-done.3.refs_5_ = bf16[256,1024]{1,0:T(8,128)(2,1)S(1)} collective-permute-done((bf16[256,1024]{1,0:T(8,128)(2,1)}, bf16[256,1024]{1,0:T(8,128)(2,1)S(1)}, u32[]{:S(2)}, u32[]{:S(2)}) %collective-permute-start.3) | collective-permute-done | bytes 524320 | tf_op jit(solution)/shard_map/ppermute | solution.py:312
  15.9 0.7 collective-permute-start.4
  16.6 5.1 %shard_map.128 = (bf16[8,64,256]{2,1,0:T(8,128)(2,1)S(1)}, bf16[8,64,256]{2,1,0:T(8,128)(2,1)S(1)}, bf16[8,64,256]{2,1,0:T(8,128)(2,1)S(1)}, bf16[8,64,256]{2,1,...) custom-call(s32[12]{0:T(128)S(1)} %compare_select_fusion.table_ref, ...), custom_call_target="tpu_custom_call" | custom-call | bytes 4194304 | tf_op jit(solution)/shard_map/pallas_call | solution.py:44
  21.8 3.8 %collective-permute-start.10 = (bf16[8,64,256]{2,1,0:T(8,128)(2,1)S(1)}, bf16[8,64,256]{2,1,0:T(8,128)(2,1)S(1)}, u32[]{:S(2)}, u32[]{:S(2)}) collective-permute-start(bf16[8,64,256]{2,1,0:T(8,128)(2,1)S(1)} %get-tuple-element.42), channel_id=1, source_target_pairs={{0,3},{1,2},{2,1},{3,0},{4,7},{5,6},{6,5},{7,4},{8,11},{9,10},{10,... | collective-permute-start | bytes 786440 | tf_op jit(solution)/shard_map/ppermute | solution.py:312
  25.6 4.6 %shard_map.129 = (bf16[8,144,256]{2,1,0:T(8,128)(2,1)S(1)}, bf16[8,144,256]{2,1,0:T(8,128)(2,1)S(1)}, bf16[8,144,256]{2,1,0:T(8,128)(2,1)S(1)}, bf16[8,144,256]{2,1,0:T(8,128)(2,1)S(1)}) custom-call(s32[12]{0:T(128)S(1)} %compare_select_fusion.table_ref, bf16[256,8192]{1,0:T(8,128)(2,1)} %bitcast.99), custom_call_target="tpu_custom_call" | custom-call | bytes 8388608 | tf_op jit(solution)/shard_map/pallas_call | solution.py:44
  30.2 0.8 copy-done.5
  31.1 1.2 collective-permute-start.11
  32.3 1.0 collective-permute-start.12
  33.3 2.2 %collective-permute-start.13 = (bf16[8,144,256]{2,1,0:T(8,128)(2,1)S(1)}, bf16[8,144,256]{2,1,0:T(8,128)(2,1)S(1)}, u32[]{:S(2)}, u32[]{:S(2)}) collective-permute-start(bf16[8,144,256]{2,1,0:T(8,128)(2,1)S(1)} %get-tuple-element.46), channel_id=1, source_target_pairs={{0,3},{1,2},{2,1},{3,0},{4,7},{5,6},{6,5},{7,4},{8,11},{9,10},{10,... | collective-permute-start | bytes 1769480 | tf_op jit(solution)/shard_map/ppermute | solution.py:312
  35.4 1.3 collective-permute-start.6
  36.7 1.3 collective-permute-start.7
  38.0 12.0 %collective-permute-done.11.refs_1_ = bf16[8,144,256]{2,1,0:T(8,128)(2,1)S(1)} collective-permute-done((bf16[8,144,256]{2,1,0:T(8,128)(2,1)S(1)}, bf16[8,144,256]{2,1,0:T(8,128)(2,1)S(1)}, u32[]{:S(2)}, u32[]{:S(2)}) %collective-permute-start.11) | collective-permute-done | bytes 589856 | tf_op jit(solution)/shard_map/ppermute | solution.py:312
  50.1 2.0 %collective-permute-start.8 = (bf16[8,64,256]{2,1,0:T(8,128)(2,1)S(1)}, bf16[8,64,256]{2,1,0:T(8,128)(2,1)S(1)}, u32[]{:S(2)}, u32[]{:S(2)}) collective-permute-start(bf16[8,64,256]{2,1,0:T(8,128)(2,1)S(1)} %get-tuple-element.40), channel_id=1, source_target_pairs={{0,1},{1,0},{2,3},{3,2},{4,5},{5,4},{6,7},{7,6},{8,9},{9,8},{10,11... | collective-permute-start | bytes 786440 | tf_op jit(solution)/shard_map/ppermute | solution.py:312
  52.1 33.6 %collective-permute-done.12.refs_2_ = bf16[8,144,256]{2,1,0:T(8,128)(2,1)S(1)} collective-permute-done((bf16[8,144,256]{2,1,0:T(8,128)(2,1)S(1)}, bf16[8,144,256]{2,1,0:T(8,128)(2,1)S(1)}, u32[]{:S(2)}, u32[]{:S(2)}) %collective-permute-start.12) | collective-permute-done | bytes 589856 | tf_op jit(solution)/shard_map/ppermute | solution.py:312
  86.4 15.3 %collective-permute-start = (bf16[8,48,256]{2,1,0:T(8,128)(2,1)S(1)}, bf16[8,48,256]{2,1,0:T(8,128)(2,1)S(1)}, u32[]{:S(2)}, u32[]{:S(2)}) collective-permute-start(bf16[8,48,256]{2,1,0:T(8,128)(2,1)S(1)} %get-tuple-element.36), channel_id=1, source_target_pairs={{0,1},{1,0},{2,3},{3,2},{4,5},{5,4},{6,7},{7,6},{8,9},{9,8},{10,11... | collective-permute-start | bytes 589832 | tf_op jit(solution)/shard_map/ppermute | solution.py:312
  101.8 1.1 collective-permute-start.1
  102.8 1.5 collective-permute-start.2
  104.3 12.4 %shard_map.130 = (f32[8,256,1024]{2,1,0:T(8,128)}, bf16[8,256,1024]{2,1,0:T(8,128)(2,1)}, bf16[8,256,1024]{2,1,0:T(8,128)(2,1)}, bf16[4,144,512]{2,1,0:T(8,128)(2,1)S(1)}, bf16[4,144,512]{2,1,0:T(8,128)(2,1)}) custom-call(s32[8]{0:T(128)S(1)} %copy-done.6, s32[1]{0:T(128)S(6)} %copy.36.step_ref, s32[12]{0:T(128)S(1)} %compare_select_fusion.table_ref, ...), custom_call_target="tpu_custom_call" | custom-call | flops 2415919104 | bytes 21233664 | tf_op jit(solution)/shard_map/pallas_call | solution.py:44
  116.8 8.2 %shard_map.131 = (f32[8,256,1024]{2,1,0:T(8,128)}, bf16[8,256,1024]{2,1,0:T(8,128)(2,1)}, bf16[8,256,1024]{2,1,0:T(8,128)(2,1)}, bf16[4,64,512]{2,1,0:T(8,128)(2,1)S(1)}, bf16[4,64,512]{2,1,0:T(8,128)(2,1)S(1)}) custom-call(s32[8]{0:T(128)S(1)} %copy-done.6, s32[1]{0:T(128)S(6)} %copy.36.step_ref, ...), custom_call_target="tpu_custom_call", output_to_operand_aliasing={{0}: (16, {}), {1}: (17, {}), {2}: (18, {})} | custom-call | flops 1073741824 | bytes 9437184 | tf_op jit(solution)/shard_map/pallas_call | solution.py:44
  125.0 5.0 %shard_map.132 = (f32[8,256,1024]{2,1,0:T(8,128)}, bf16[8,256,1024]{2,1,0:T(8,128)(2,1)}, bf16[8,256,1024]{2,1,0:T(8,128)(2,1)}, bf16[4,48,512]{2,1,0:T(8,128)(2,1)S(1)}, bf16[4,48,512]{2,1,0:T(8,128)(2,1)S(1)}) custom-call(s32[8]{0:T(128)S(1)} %copy-done.6, s32[1]{0:T(128)S(6)} %copy.36.step_ref, ...), custom_call_target="tpu_custom_call", output_to_operand_aliasing={{0}: (16, {}), {1}: (17, {}), {2}: (18, {})} | custom-call | flops 402653184 | bytes 3932160 | tf_op jit(solution)/shard_map/pallas_call | solution.py:44
  130.1 0.1 collective-permute-start.14
  130.1 1.4 collective-permute-done.14
  131.7 1.6 collective-permute-start.15
  133.2 1.5 collective-permute-start.16
  134.7 0.5 collective-permute-start.17
  135.2 0.5 collective-permute-start.22
  135.7 0.1 collective-permute-done.15
  135.8 1.5 collective-permute-done.16
  137.3 2.4 %collective-permute-done.17 = bf16[48,512]{1,0:T(8,128)(2,1)S(1)} collective-permute-done((bf16[48,512]{1,0:T(8,128)(2,1)S(1)}, bf16[48,512]{1,0:T(8,128)(2,1)S(1)}, u32[]{:S(2)}, u32[]{:S(2)}) %collective-permute-start.17) | collective-permute-done | bytes 49184 | tf_op jit(solution)/shard_map/ppermute | solution.py:312
  139.8 0.1 convert_add_fusion.1
  139.9 0.6 collective-permute-start.31
  140.5 0.5 collective-permute-start.32
  141.0 2.4 %collective-permute-start.33 = (bf16[64,512]{1,0:T(8,128)(2,1)S(1)}, bf16[64,512]{1,0:T(8,128)(2,1)S(1)}, u32[]{:S(2)}, u32[]{:S(2)}) collective-permute-start(bf16[64,512]{1,0:T(8,128)(2,1)S(1)} %get-tuple-element.87), channel_id=1, source_target_pairs={{0,24},{4,28},{8,16},{12,20},{16,8},{20,12},{24,0},{28,4},{1,25},{... | collective-permute-start | bytes 196616 | tf_op jit(solution)/shard_map/ppermute | solution.py:312
  143.5 0.2 convert_add_fusion
  143.7 0.6 collective-permute-start.23
  144.3 0.5 collective-permute-start.24
  144.8 2.4 %collective-permute-start.25 = (bf16[144,512]{1,0:T(8,128)(2,1)S(1)}, bf16[144,512]{1,0:T(8,128)(2,1)S(1)}, u32[]{:S(2)}, u32[]{:S(2)}) collective-permute-start(bf16[144,512]{1,0:T(8,128)(2,1)S(1)} %get-tuple-element.80), channel_id=1, source_target_pairs={{0,24},{4,28},{8,16},{12,20},{16,8},{20,12},{24,0},{28,4},{1,25},{... | collective-permute-start | bytes 442376 | tf_op jit(solution)/shard_map/ppermute | solution.py:312
  147.4 2.3 %collective-permute-done.23 = bf16[144,512]{1,0:T(8,128)(2,1)S(1)} collective-permute-done((bf16[144,512]{1,0:T(8,128)(2,1)S(1)}, bf16[144,512]{1,0:T(8,128)(2,1)S(1)}, u32[]{:S(2)}, u32[]{:S(2)}) %collective-permute-start.23) | collective-permute-done | bytes 147488 | tf_op jit(solution)/shard_map/ppermute | solution.py:312
  149.7 2.1 %collective-permute-done.24 = bf16[144,512]{1,0:T(8,128)(2,1)S(1)} collective-permute-done((bf16[144,512]{1,0:T(8,128)(2,1)S(1)}, bf16[144,512]{1,0:T(8,128)(2,1)S(1)}, u32[]{:S(2)}, u32[]{:S(2)}) %collective-permute-start.24) | collective-permute-done | bytes 147488 | tf_op jit(solution)/shard_map/ppermute | solution.py:312
  151.8 0.1 multiply_add_fusion
  151.9 0.1 fusion.22
  152.1 1.6 collective-permute-start.26
  153.6 0.8 collective-permute-start.27
  154.4 1.2 collective-permute-start.28
  155.7 1.6 collective-permute-start.34
  157.2 0.8 collective-permute-start.35
  158.0 0.8 collective-permute-done.26
  158.8 1.1 collective-permute-start.36
  160.0 1.1 collective-permute-done.27
  161.0 0.1 pad_maximum_fusion.refs_0_
  161.1 0.1 collective-permute-start.29
  161.2 0.6 collective-permute-start.18
  161.9 1.1 collective-permute-start.19
  163.0 1.8 %collective-permute-start.20 = (bf16[48,512]{1,0:T(8,128)(2,1)S(1)}, bf16[48,512]{1,0:T(8,128)(2,1)S(1)}, u32[]{:S(2)}, u32[]{:S(2)}) collective-permute-start(bf16[48,512]{1,0:T(8,128)(2,1)S(1)} %get-tuple-element.75), channel_id=1, source_target_pairs={{0,24},{4,28},{8,16},{12,20},{16,8},{20,12},{24,0},{28,4},{1,25},{... | collective-permute-start | bytes 147464 | tf_op jit(solution)/shard_map/ppermute | solution.py:312
  164.8 0.1 collective-permute-start.37
  164.9 0.5 collective-permute-done.18
  165.4 0.5 collective-permute-done.19
  166.0 2.0 %collective-permute-done.20 = bf16[48,512]{1,0:T(8,128)(2,1)S(1)} collective-permute-done((bf16[48,512]{1,0:T(8,128)(2,1)S(1)}, bf16[48,512]{1,0:T(8,128)(2,1)S(1)}, u32[]{:S(2)}, u32[]{:S(2)}) %collective-permute-start.20) | collective-permute-done | bytes 49184 | tf_op jit(solution)/shard_map/ppermute | solution.py:312
  168.1 4.7 %shard_map.133 = (f32[8,256,1024]{2,1,0:T(8,128)}, bf16[8,256,1024]{2,1,0:T(8,128)(2,1)}, bf16[8,256,1024]{2,1,0:T(8,128)(2,1)}) custom-call(s32[8]{0:T(128)S(1)} %copy-done.6, s32[1]{0:T(128)S(6)} %copy.36.step_ref, s32[12]{0:T(128)S(1)} %compare_select_fusion.table_ref, ...), custom_call_target="tpu_custom_call", output_to_operand_aliasing={{0}: (16, {}), {1}: (17, {}), {2}: (18, {})} | custom-call | flops 402653184 | bytes 3932160 | tf_op jit(solution)/shard_map/pallas_call | solution.py:44
  172.8 1.0 pad_maximum_fusion.1
  173.8 2.4 %shard_map.134.refs_2_ = f32[8,256,1024]{2,1,0:T(8,128)} custom-call(s32[8]{0:T(128)S(1)} %copy-done.6, s32[1]{0:T(128)S(6)} %copy.36.step_ref, s32[12]{0:T(128)S(1)} %compare_select_fusion.table_ref, bf16[4,144,512]{2,1,0:T(8,128)(2,1)S(1)} %pad_maximum_fusion.refs_0_, ...), custom_call_target="tpu_custom_call", output_to_operand_aliasing={{}: (7, {})} | custom-call | bytes 6815744 | tf_op jit(solution)/shard_map/pallas_call | solution.py:44
  176.2 1.5 shard_map.135
  (63 shorter events, 0.6 us)
Async XLA Ops:
  0.6 15.3 %collective-permute-start.3 = (bf16[256,1024]{1,0:T(8,128)(2,1)}, bf16[256,1024]{1,0:T(8,128)(2,1)S(1)}, u32[]{:S(2)}, u32[]{:S(2)}) collective-permute-start(bf16[256,1024]{1,0:T(8,128)(2,1)} %bitcast.77), channel_id=1, source_target_pairs={{0,1},{1,0},{2,3},{3,2},{4,5},{5,4},{6,7},{7,6},{8,9},{9,8},{10,11... | collective-permute-start | bytes 1572872 | tf_op jit(solution)/shard_map/ppermute | solution.py:312
  3.7 31.7 %collective-permute-start.5 = (bf16[256,1024]{1,0:T(8,128)(2,1)}, bf16[256,1024]{1,0:T(8,128)(2,1)S(1)}, u32[]{:S(2)}, u32[]{:S(2)}) collective-permute-start(bf16[256,1024]{1,0:T(8,128)(2,1)} %bitcast.78), channel_id=1, source_target_pairs={{1,2},{2,1},{5,6},{6,5},{9,10},{10,9},{13,14},{14,13},{17,18},{18,... | collective-permute-start | bytes 1572872 | tf_op jit(solution)/shard_map/ppermute | solution.py:318
  15.9 20.9 %collective-permute-start.4 = (bf16[256,1024]{1,0:T(8,128)(2,1)S(1)}, bf16[256,1024]{1,0:T(8,128)(2,1)S(1)}, u32[]{:S(2)}, u32[]{:S(2)}) collective-permute-start(bf16[256,1024]{1,0:T(8,128)(2,1)S(1)} %collective-permute-done.3.refs_5_), channel_id=1, source_target_pairs={{1,2},{2,1},{5,6},{6,5},{9,10},{10,9},{13,14},{14,13},{17,18},{18,... | collective-permute-start | bytes 1572872 | tf_op jit(solution)/shard_map/ppermute | solution.py:319
  16.6 87.7 %copy-start = (bf16[1,256,1024]{2,1,0:T(8,128)(2,1)S(1)}, bf16[1,256,1024]{2,1,0:T(8,128)(2,1)}, u32[]{:S(2)}) copy-start(bf16[1,256,1024]{2,1,0:T(8,128)(2,1)} %param.10) | copy-start | bytes 1572868
  16.6 87.7 %copy-start.6 = (s32[8]{0:T(128)S(1)}, s32[8]{0:T(128)}, u32[]{:S(2)}) copy-start(s32[8]{0:T(128)} %heads_ref.11) | copy-start | bytes 100
  21.8 11.5 %collective-permute-start.10 = (bf16[8,64,256]{2,1,0:T(8,128)(2,1)S(1)}, bf16[8,64,256]{2,1,0:T(8,128)(2,1)S(1)}, u32[]{:S(2)}, u32[]{:S(2)}) collective-permute-start(bf16[8,64,256]{2,1,0:T(8,128)(2,1)S(1)} %get-tuple-element.42), channel_id=1, source_target_pairs={{0,3},{1,2},{2,1},{3,0},{4,7},{5,6},{6,5},{7,4},{8,11},{9,10},{10,... | collective-permute-start | bytes 786440 | tf_op jit(solution)/shard_map/ppermute | solution.py:312
  30.2 0.8 copy-start.5
  31.1 19.0 %collective-permute-start.11 = (bf16[8,144,256]{2,1,0:T(8,128)(2,1)S(1)}, bf16[8,144,256]{2,1,0:T(8,128)(2,1)S(1)}, u32[]{:S(2)}, u32[]{:S(2)}) collective-permute-start(bf16[8,144,256]{2,1,0:T(8,128)(2,1)S(1)} %get-tuple-element.44), channel_id=1, source_target_pairs={{0,1},{1,0},{2,3},{3,2},{4,5},{5,4},{6,7},{7,6},{8,9},{9,8},{10,11... | collective-permute-start | bytes 1769480 | tf_op jit(solution)/shard_map/ppermute | solution.py:312
  32.3 53.5 %collective-permute-start.12 = (bf16[8,144,256]{2,1,0:T(8,128)(2,1)S(1)}, bf16[8,144,256]{2,1,0:T(8,128)(2,1)S(1)}, u32[]{:S(2)}, u32[]{:S(2)}) collective-permute-start(bf16[8,144,256]{2,1,0:T(8,128)(2,1)S(1)} %get-tuple-element.45), channel_id=1, source_target_pairs={{0,2},{1,3},{2,0},{3,1},{4,6},{5,7},{6,4},{7,5},{8,10},{9,11},{10,... | collective-permute-start | bytes 1769480 | tf_op jit(solution)/shard_map/ppermute | solution.py:312
  33.3 53.1 %collective-permute-start.13 = (bf16[8,144,256]{2,1,0:T(8,128)(2,1)S(1)}, bf16[8,144,256]{2,1,0:T(8,128)(2,1)S(1)}, u32[]{:S(2)}, u32[]{:S(2)}) collective-permute-start(bf16[8,144,256]{2,1,0:T(8,128)(2,1)S(1)} %get-tuple-element.46), channel_id=1, source_target_pairs={{0,3},{1,2},{2,1},{3,0},{4,7},{5,6},{6,5},{7,4},{8,11},{9,10},{10,... | collective-permute-start | bytes 1769480 | tf_op jit(solution)/shard_map/ppermute | solution.py:312
  35.4 81.3 %copy-start.1 = (bf16[256,1024]{1,0:T(8,128)(2,1)}, bf16[256,1024]{1,0:T(8,128)(2,1)S(1)}, u32[]{:S(2)}) copy-start(bf16[256,1024]{1,0:T(8,128)(2,1)S(1)} %collective-permute-done.5.refs_8_) | copy-start | bytes 1572868
  35.4 66.3 %collective-permute-start.6 = (bf16[256,1024]{1,0:T(8,128)(2,1)S(1)}, bf16[256,1024]{1,0:T(8,128)(2,1)S(1)}, u32[]{:S(2)}, u32[]{:S(2)}) collective-permute-start(bf16[256,1024]{1,0:T(8,128)(2,1)S(1)} %collective-permute-done.5.refs_8_), channel_id=1, source_target_pairs={{1,0},{2,3},{5,4},{6,7},{9,8},{10,11},{13,12},{14,15},{17,16},{18,... | collective-permute-start | bytes 1572872 | tf_op jit(solution)/shard_map/ppermute | solution.py:320
  36.7 66.1 %collective-permute-start.7 = (bf16[256,1024]{1,0:T(8,128)(2,1)S(1)}, bf16[256,1024]{1,0:T(8,128)(2,1)S(1)}, u32[]{:S(2)}, u32[]{:S(2)}) collective-permute-start(bf16[256,1024]{1,0:T(8,128)(2,1)S(1)} %collective-permute-done.4.refs_6_), channel_id=1, source_target_pairs={{1,0},{2,3},{5,4},{6,7},{9,8},{10,11},{13,12},{14,15},{17,16},{18,... | collective-permute-start | bytes 1572872 | tf_op jit(solution)/shard_map/ppermute | solution.py:321
  50.1 54.2 %copy-start.9 = (bf16[8,144,256]{2,1,0:T(8,128)(2,1)}, bf16[8,144,256]{2,1,0:T(8,128)(2,1)S(1)}, u32[]{:S(2)}) copy-start(bf16[8,144,256]{2,1,0:T(8,128)(2,1)S(1)} %collective-permute-done.11.refs_1_) | copy-start | bytes 1769476
  50.1 66.6 %collective-permute-start.8 = (bf16[8,64,256]{2,1,0:T(8,128)(2,1)S(1)}, bf16[8,64,256]{2,1,0:T(8,128)(2,1)S(1)}, u32[]{:S(2)}, u32[]{:S(2)}) collective-permute-start(bf16[8,64,256]{2,1,0:T(8,128)(2,1)S(1)} %get-tuple-element.40), channel_id=1, source_target_pairs={{0,1},{1,0},{2,3},{3,2},{4,5},{5,4},{6,7},{7,6},{8,9},{9,8},{10,11... | collective-permute-start | bytes 786440 | tf_op jit(solution)/shard_map/ppermute | solution.py:312
  85.7 18.6 %copy-start.10 = (bf16[8,144,256]{2,1,0:T(8,128)(2,1)}, bf16[8,144,256]{2,1,0:T(8,128)(2,1)S(1)}, u32[]{:S(2)}) copy-start(bf16[8,144,256]{2,1,0:T(8,128)(2,1)S(1)} %collective-permute-done.12.refs_2_) | copy-start | bytes 1769476
  85.7 31.0 %collective-permute-start.9 = (bf16[8,64,256]{2,1,0:T(8,128)(2,1)S(1)}, bf16[8,64,256]{2,1,0:T(8,128)(2,1)S(1)}, u32[]{:S(2)}, u32[]{:S(2)}) collective-permute-start(bf16[8,64,256]{2,1,0:T(8,128)(2,1)S(1)} %get-tuple-element.41), channel_id=1, source_target_pairs={{0,2},{1,3},{2,0},{3,1},{4,6},{5,7},{6,4},{7,5},{8,10},{9,11},{10,... | collective-permute-start | bytes 786440 | tf_op jit(solution)/shard_map/ppermute | solution.py:312
  86.4 17.9 %copy-start.11 = (bf16[8,144,256]{2,1,0:T(8,128)(2,1)}, bf16[8,144,256]{2,1,0:T(8,128)(2,1)S(1)}, u32[]{:S(2)}) copy-start(bf16[8,144,256]{2,1,0:T(8,128)(2,1)S(1)} %collective-permute-done.13.refs_3_) | copy-start | bytes 1769476
  86.4 38.5 %collective-permute-start = (bf16[8,48,256]{2,1,0:T(8,128)(2,1)S(1)}, bf16[8,48,256]{2,1,0:T(8,128)(2,1)S(1)}, u32[]{:S(2)}, u32[]{:S(2)}) collective-permute-start(bf16[8,48,256]{2,1,0:T(8,128)(2,1)S(1)} %get-tuple-element.36), channel_id=1, source_target_pairs={{0,1},{1,0},{2,3},{3,2},{4,5},{5,4},{6,7},{7,6},{8,9},{9,8},{10,11... | collective-permute-start | bytes 589832 | tf_op jit(solution)/shard_map/ppermute | solution.py:312
  101.8 23.2 %collective-permute-start.1 = (bf16[8,48,256]{2,1,0:T(8,128)(2,1)S(1)}, bf16[8,48,256]{2,1,0:T(8,128)(2,1)S(1)}, u32[]{:S(2)}, u32[]{:S(2)}) collective-permute-start(bf16[8,48,256]{2,1,0:T(8,128)(2,1)S(1)} %get-tuple-element.37), channel_id=1, source_target_pairs={{0,2},{1,3},{2,0},{3,1},{4,6},{5,7},{6,4},{7,5},{8,10},{9,11},{10,... | collective-permute-start | bytes 589832 | tf_op jit(solution)/shard_map/ppermute | solution.py:312
  102.8 13.9 %copy-start.3 = (bf16[256,1024]{1,0:T(8,128)(2,1)}, bf16[256,1024]{1,0:T(8,128)(2,1)S(1)}, u32[]{:S(2)}) copy-start(bf16[256,1024]{1,0:T(8,128)(2,1)S(1)} %collective-permute-done.7.refs_9_) | copy-start | bytes 1572868
  102.8 22.1 %collective-permute-start.2 = (bf16[8,48,256]{2,1,0:T(8,128)(2,1)S(1)}, bf16[8,48,256]{2,1,0:T(8,128)(2,1)S(1)}, u32[]{:S(2)}, u32[]{:S(2)}) collective-permute-start(bf16[8,48,256]{2,1,0:T(8,128)(2,1)S(1)} %get-tuple-element.38), channel_id=1, source_target_pairs={{0,3},{1,2},{2,1},{3,0},{4,7},{5,6},{6,5},{7,4},{8,11},{9,10},{10,... | collective-permute-start | bytes 589832 | tf_op jit(solution)/shard_map/ppermute | solution.py:312
  116.7 8.2 %copy-start.2 = (bf16[256,1024]{1,0:T(8,128)(2,1)S(1)}, bf16[256,1024]{1,0:T(8,128)(2,1)}, u32[]{:S(2)}) copy-start(bf16[256,1024]{1,0:T(8,128)(2,1)} %copy-done.1) | copy-start | bytes 1572868
  125.0 10.2 %copy-start.12 = (bf16[4,144,512]{2,1,0:T(8,128)(2,1)S(1)}, bf16[4,144,512]{2,1,0:T(8,128)(2,1)}, u32[]{:S(2)}) copy-start(bf16[4,144,512]{2,1,0:T(8,128)(2,1)} %get-tuple-element.56) | copy-start | bytes 1769476
  125.0 14.7 %copy-start.7 = (f32[256,512]{1,0:T(8,128)S(1)}, f32[256,512]{1,0:T(8,128)}, u32[]{:S(2)}) copy-start(f32[256,512]{1,0:T(8,128)} %param.15) | copy-start | bytes 1572868
  125.0 14.7 %copy-start.8 = (f32[256,512]{1,0:T(8,128)S(1)}, f32[256,512]{1,0:T(8,128)}, u32[]{:S(2)}) copy-start(f32[256,512]{1,0:T(8,128)} %param.14) | copy-start | bytes 1572868
  130.1 1.5 collective-permute-start.14
  131.7 4.2 %collective-permute-start.15 = (bf16[48,512]{1,0:T(8,128)(2,1)S(1)}, bf16[48,512]{1,0:T(8,128)(2,1)S(1)}, u32[]{:S(2)}, u32[]{:S(2)}) collective-permute-start(bf16[48,512]{1,0:T(8,128)(2,1)S(1)} %get-tuple-element.89), channel_id=1, source_target_pairs={{0,8},{4,12},{8,0},{12,4},{16,24},{20,28},{24,16},{28,20},{1,9},{5... | collective-permute-start | bytes 147464 | tf_op jit(solution)/shard_map/ppermute | solution.py:312
  133.2 4.1 %collective-permute-start.16 = (bf16[48,512]{1,0:T(8,128)(2,1)S(1)}, bf16[48,512]{1,0:T(8,128)(2,1)S(1)}, u32[]{:S(2)}, u32[]{:S(2)}) collective-permute-start(bf16[48,512]{1,0:T(8,128)(2,1)S(1)} %get-tuple-element.91), channel_id=1, source_target_pairs={{0,16},{4,20},{8,24},{12,28},{16,0},{20,4},{24,8},{28,12},{1,17},{... | collective-permute-start | bytes 147464 | tf_op jit(solution)/shard_map/ppermute | solution.py:312
  134.7 5.0 %collective-permute-start.17 = (bf16[48,512]{1,0:T(8,128)(2,1)S(1)}, bf16[48,512]{1,0:T(8,128)(2,1)S(1)}, u32[]{:S(2)}, u32[]{:S(2)}) collective-permute-start(bf16[48,512]{1,0:T(8,128)(2,1)S(1)} %get-tuple-element.90), channel_id=1, source_target_pairs={{0,24},{4,28},{8,16},{12,20},{16,8},{20,12},{24,0},{28,4},{1,25},{... | collective-permute-start | bytes 147464 | tf_op jit(solution)/shard_map/ppermute | solution.py:312
  135.2 4.6 %collective-permute-start.30 = (bf16[4,64,512]{2,1,0:T(8,128)(2,1)S(1)}, bf16[4,64,512]{2,1,0:T(8,128)(2,1)S(1)}, u32[]{:S(2)}, u32[]{:S(2)}) collective-permute-start(bf16[4,64,512]{2,1,0:T(8,128)(2,1)S(1)} %get-tuple-element.58), channel_id=1, source_target_pairs={{0,4},{4,0},{8,12},{12,8},{16,20},{20,16},{24,28},{28,24},{1,5},{5... | collective-permute-start | bytes 786440 | tf_op jit(solution)/shard_map/ppermute | solution.py:312
  135.2 8.2 %collective-permute-start.22 = (bf16[4,144,512]{2,1,0:T(8,128)(2,1)S(1)}, bf16[4,144,512]{2,1,0:T(8,128)(2,1)S(1)}, u32[]{:S(2)}, u32[]{:S(2)}) collective-permute-start(bf16[4,144,512]{2,1,0:T(8,128)(2,1)S(1)} %copy-done.12), channel_id=1, source_target_pairs={{0,4},{4,0},{8,12},{12,8},{16,20},{20,16},{24,28},{28,24},{1,5},{5... | collective-permute-start | bytes 1769480 | tf_op jit(solution)/shard_map/ppermute | solution.py:312
  139.9 4.9 %collective-permute-start.31 = (bf16[64,512]{1,0:T(8,128)(2,1)S(1)}, bf16[64,512]{1,0:T(8,128)(2,1)S(1)}, u32[]{:S(2)}, u32[]{:S(2)}) collective-permute-start(bf16[64,512]{1,0:T(8,128)(2,1)S(1)} %get-tuple-element.86), channel_id=1, source_target_pairs={{0,8},{4,12},{8,0},{12,4},{16,24},{20,28},{24,16},{28,20},{1,9},{5... | collective-permute-start | bytes 196616 | tf_op jit(solution)/shard_map/ppermute | solution.py:312
  140.5 6.8 %collective-permute-start.32 = (bf16[64,512]{1,0:T(8,128)(2,1)S(1)}, bf16[64,512]{1,0:T(8,128)(2,1)S(1)}, u32[]{:S(2)}, u32[]{:S(2)}) collective-permute-start(bf16[64,512]{1,0:T(8,128)(2,1)S(1)} %get-tuple-element.88), channel_id=1, source_target_pairs={{0,16},{4,20},{8,24},{12,28},{16,0},{20,4},{24,8},{28,12},{1,17},{... | collective-permute-start | bytes 196616 | tf_op jit(solution)/shard_map/ppermute | solution.py:312
  141.0 6.3 %collective-permute-start.33 = (bf16[64,512]{1,0:T(8,128)(2,1)S(1)}, bf16[64,512]{1,0:T(8,128)(2,1)S(1)}, u32[]{:S(2)}, u32[]{:S(2)}) collective-permute-start(bf16[64,512]{1,0:T(8,128)(2,1)S(1)} %get-tuple-element.87), channel_id=1, source_target_pairs={{0,24},{4,28},{8,16},{12,20},{16,8},{20,12},{24,0},{28,4},{1,25},{... | collective-permute-start | bytes 196616 | tf_op jit(solution)/shard_map/ppermute | solution.py:312
  143.7 24.4 %copy-start.4 = (bf16[256,1024]{1,0:T(8,128)(2,1)S(1)}, bf16[256,1024]{1,0:T(8,128)(2,1)}, u32[]{:S(2)}) copy-start(bf16[256,1024]{1,0:T(8,128)(2,1)} %copy-done.3) | copy-start | bytes 1572868
  143.7 6.0 %collective-permute-start.23 = (bf16[144,512]{1,0:T(8,128)(2,1)S(1)}, bf16[144,512]{1,0:T(8,128)(2,1)S(1)}, u32[]{:S(2)}, u32[]{:S(2)}) collective-permute-start(bf16[144,512]{1,0:T(8,128)(2,1)S(1)} %get-tuple-element.79), channel_id=1, source_target_pairs={{0,8},{4,12},{8,0},{12,4},{16,24},{20,28},{24,16},{28,20},{1,9},{5... | collective-permute-start | bytes 442376 | tf_op jit(solution)/shard_map/ppermute | solution.py:312
  144.3 7.5 %collective-permute-start.24 = (bf16[144,512]{1,0:T(8,128)(2,1)S(1)}, bf16[144,512]{1,0:T(8,128)(2,1)S(1)}, u32[]{:S(2)}, u32[]{:S(2)}) collective-permute-start(bf16[144,512]{1,0:T(8,128)(2,1)S(1)} %get-tuple-element.81), channel_id=1, source_target_pairs={{0,16},{4,20},{8,24},{12,28},{16,0},{20,4},{24,8},{28,12},{1,17},{... | collective-permute-start | bytes 442376 | tf_op jit(solution)/shard_map/ppermute | solution.py:312
  144.8 6.9 %collective-permute-start.25 = (bf16[144,512]{1,0:T(8,128)(2,1)S(1)}, bf16[144,512]{1,0:T(8,128)(2,1)S(1)}, u32[]{:S(2)}, u32[]{:S(2)}) collective-permute-start(bf16[144,512]{1,0:T(8,128)(2,1)S(1)} %get-tuple-element.80), channel_id=1, source_target_pairs={{0,24},{4,28},{8,16},{12,20},{16,8},{20,12},{24,0},{28,4},{1,25},{... | collective-permute-start | bytes 442376 | tf_op jit(solution)/shard_map/ppermute | solution.py:312
  152.1 6.8 %collective-permute-start.26 = (bf16[144,512]{1,0:T(8,128)(2,1)S(1)}, bf16[144,512]{1,0:T(8,128)(2,1)S(1)}, u32[]{:S(2)}, u32[]{:S(2)}) collective-permute-start(bf16[144,512]{1,0:T(8,128)(2,1)S(1)} %get-tuple-element.73), channel_id=1, source_target_pairs={{0,8},{4,12},{8,0},{12,4},{16,24},{20,28},{24,16},{28,20},{1,9},{5... | collective-permute-start | bytes 442376 | tf_op jit(solution)/shard_map/ppermute | solution.py:312
  153.6 7.4 %collective-permute-start.27 = (bf16[144,512]{1,0:T(8,128)(2,1)S(1)}, bf16[144,512]{1,0:T(8,128)(2,1)S(1)}, u32[]{:S(2)}, u32[]{:S(2)}) collective-permute-start(bf16[144,512]{1,0:T(8,128)(2,1)S(1)} %get-tuple-element.73), channel_id=1, source_target_pairs={{0,16},{4,20},{8,24},{12,28},{16,0},{20,4},{24,8},{28,12},{1,17},{... | collective-permute-start | bytes 442376 | tf_op jit(solution)/shard_map/ppermute | solution.py:312
  154.4 6.6 %collective-permute-start.28 = (bf16[144,512]{1,0:T(8,128)(2,1)S(1)}, bf16[144,512]{1,0:T(8,128)(2,1)S(1)}, u32[]{:S(2)}, u32[]{:S(2)}) collective-permute-start(bf16[144,512]{1,0:T(8,128)(2,1)S(1)} %get-tuple-element.73), channel_id=1, source_target_pairs={{0,24},{4,28},{8,16},{12,20},{16,8},{20,12},{24,0},{28,4},{1,25},{... | collective-permute-start | bytes 442376 | tf_op jit(solution)/shard_map/ppermute | solution.py:312
  155.7 6.2 %collective-permute-start.34 = (bf16[64,512]{1,0:T(8,128)(2,1)S(1)}, bf16[64,512]{1,0:T(8,128)(2,1)S(1)}, u32[]{:S(2)}, u32[]{:S(2)}) collective-permute-start(bf16[64,512]{1,0:T(8,128)(2,1)S(1)} %get-tuple-element.71), channel_id=1, source_target_pairs={{0,8},{4,12},{8,0},{12,4},{16,24},{20,28},{24,16},{28,20},{1,9},{5... | collective-permute-start | bytes 196616 | tf_op jit(solution)/shard_map/ppermute | solution.py:312
  157.2 5.8 %collective-permute-start.35 = (bf16[64,512]{1,0:T(8,128)(2,1)S(1)}, bf16[64,512]{1,0:T(8,128)(2,1)S(1)}, u32[]{:S(2)}, u32[]{:S(2)}) collective-permute-start(bf16[64,512]{1,0:T(8,128)(2,1)S(1)} %get-tuple-element.71), channel_id=1, source_target_pairs={{0,16},{4,20},{8,24},{12,28},{16,0},{20,4},{24,8},{28,12},{1,17},{... | collective-permute-start | bytes 196616 | tf_op jit(solution)/shard_map/ppermute | solution.py:312
  158.8 6.0 %collective-permute-start.36 = (bf16[64,512]{1,0:T(8,128)(2,1)S(1)}, bf16[64,512]{1,0:T(8,128)(2,1)S(1)}, u32[]{:S(2)}, u32[]{:S(2)}) collective-permute-start(bf16[64,512]{1,0:T(8,128)(2,1)S(1)} %get-tuple-element.71), channel_id=1, source_target_pairs={{0,24},{4,28},{8,16},{12,20},{16,8},{20,12},{24,0},{28,4},{1,25},{... | collective-permute-start | bytes 196616 | tf_op jit(solution)/shard_map/ppermute | solution.py:312
  161.1 12.7 %collective-permute-start.29 = (bf16[4,144,512]{2,1,0:T(8,128)(2,1)S(1)}, bf16[4,144,512]{2,1,0:T(8,128)(2,1)S(1)}, u32[]{:S(2)}, u32[]{:S(2)}) collective-permute-start(bf16[4,144,512]{2,1,0:T(8,128)(2,1)S(1)} %pad_maximum_fusion.refs_0_), channel_id=1, source_target_pairs={{0,4},{4,0},{8,12},{12,8},{16,20},{20,16},{24,28},{28,24},{1,5},{5... | collective-permute-start | bytes 1769480 | tf_op jit(solution)/shard_map/ppermute | solution.py:312
  161.2 4.2 %collective-permute-start.18 = (bf16[48,512]{1,0:T(8,128)(2,1)S(1)}, bf16[48,512]{1,0:T(8,128)(2,1)S(1)}, u32[]{:S(2)}, u32[]{:S(2)}) collective-permute-start(bf16[48,512]{1,0:T(8,128)(2,1)S(1)} %get-tuple-element.75), channel_id=1, source_target_pairs={{0,8},{4,12},{8,0},{12,4},{16,24},{20,28},{24,16},{28,20},{1,9},{5... | collective-permute-start | bytes 147464 | tf_op jit(solution)/shard_map/ppermute | solution.py:312
  161.9 4.1 %collective-permute-start.19 = (bf16[48,512]{1,0:T(8,128)(2,1)S(1)}, bf16[48,512]{1,0:T(8,128)(2,1)S(1)}, u32[]{:S(2)}, u32[]{:S(2)}) collective-permute-start(bf16[48,512]{1,0:T(8,128)(2,1)S(1)} %get-tuple-element.75), channel_id=1, source_target_pairs={{0,16},{4,20},{8,24},{12,28},{16,0},{20,4},{24,8},{28,12},{1,17},{... | collective-permute-start | bytes 147464 | tf_op jit(solution)/shard_map/ppermute | solution.py:312
  163.0 5.0 %collective-permute-start.20 = (bf16[48,512]{1,0:T(8,128)(2,1)S(1)}, bf16[48,512]{1,0:T(8,128)(2,1)S(1)}, u32[]{:S(2)}, u32[]{:S(2)}) collective-permute-start(bf16[48,512]{1,0:T(8,128)(2,1)S(1)} %get-tuple-element.75), channel_id=1, source_target_pairs={{0,24},{4,28},{8,16},{12,20},{16,8},{20,12},{24,0},{28,4},{1,25},{... | collective-permute-start | bytes 147464 | tf_op jit(solution)/shard_map/ppermute | solution.py:312
  164.8 9.0 %collective-permute-start.37 = (bf16[4,64,512]{2,1,0:T(8,128)(2,1)S(1)}, bf16[4,64,512]{2,1,0:T(8,128)(2,1)S(1)}, u32[]{:S(2)}, u32[]{:S(2)}) collective-permute-start(bf16[4,64,512]{2,1,0:T(8,128)(2,1)S(1)} %pad_maximum_fusion.3.refs_2_), channel_id=1, source_target_pairs={{0,4},{4,0},{8,12},{12,8},{16,20},{20,16},{24,28},{28,24},{1,5},{5... | collective-permute-start | bytes 786440 | tf_op jit(solution)/shard_map/ppermute | solution.py:312
  168.0 8.2 %collective-permute-start.21 = (bf16[4,48,512]{2,1,0:T(8,128)(2,1)S(1)}, bf16[4,48,512]{2,1,0:T(8,128)(2,1)S(1)}, u32[]{:S(2)}, u32[]{:S(2)}) collective-permute-start(bf16[4,48,512]{2,1,0:T(8,128)(2,1)S(1)} %pad_maximum_fusion.4.refs_0_), channel_id=1, source_target_pairs={{0,4},{4,0},{8,12},{12,8},{16,20},{20,16},{24,28},{28,24},{1,5},{5... | collective-permute-start | bytes 589832 | tf_op jit(solution)/shard_map/ppermute | solution.py:312

commit v2 on v1

--- a/solution.py
+++ b/solution.py
@@ -35,7 +35,7 @@
     return pl.ds(pl.multiple_of(head_at(heads_ref, step_ref, position) * HD, HD), HD)
 
 
-VMEM_GRANT = 67043328 - 56 * 2**18
+VMEM_GRANT = 67043328 - 68 * 2**18
 
 
 def call(
@@ -322,20 +322,23 @@
     return [own, near, next_far, relay, far, next_relay]
 
 
-def island_sum(keep, give):
+def island_trade(keep, give, waiting):
     got = swap(give, "island", 1)
     part = keep.astype(jnp.float32) + got.astype(jnp.float32)
-    total = part[0]
+    total, rows = part[0], [waiting]
+    ahead = 0 if waiting is None else waiting.shape[0]
     for d in range(1, part.shape[0]):
         piece = part[d].astype(jnp.bfloat16)
-        total = total + swap(piece, "island", 2 * d).astype(jnp.float32)
-    return total
-
-
-def island_spread(own):
-    chips = lax.axis_size("island") // 2
-    pieces = [own] + [swap(own, "island", 2 * d) for d in range(1, chips)]
-    near = jnp.stack(pieces)
+        if ahead:
+            piece = jnp.concatenate([waiting, piece])
+        piece = swap(piece, "island", 2 * d)
+        rows.append(piece[:ahead])
+        total = total + piece[ahead:].astype(jnp.float32)
+    return total, rows
+
+
+def island_rows(rows):
+    near = jnp.stack(rows)
     return near, swap(near, "island", 1)
 
 
@@ -379,7 +382,7 @@
     ]
 
     state = [a[0].reshape(islands, span, width) for a in (params, first_moment, second_moment)]
-    olds = None
+    olds = waiting = None
     bases, momenta, news = [], [], []
 
     def run(c, place):
@@ -391,11 +394,17 @@
         else:
             olds, pieces = run(c, (0, SYNC))
             olds, _ = run(c, (SYNC, KVH - SYNC))
-        total = island_sum(*pieces)
+        total, rows_in = island_trade(*pieces, waiting)
+        if c:
+            news.append(island_rows(rows_in))
         new, mom = outer_update(base[k0 : k0 + w], outer_momentum[k0 : k0 + w], total, islands)
         bases.append(new)
         momenta.append(mom)
-        news.append(island_spread(new.astype(jnp.bfloat16)))
+        waiting = new.astype(jnp.bfloat16)
+    rows_in = [waiting]
+    for d in range(1, islands // 2):
+        rows_in.append(swap(waiting, "island", 2 * d))
+    news.append(island_rows(rows_in))
     starts = [k0 for k0, _ in plan]
     out = place_base(*hs, table, news[:last], olds[0], starts[:last])
     out = place_base(*hs, table, news[last:], out, starts[last:])

time: 178 us -> 180 us (1.011)
  waiting for transfers between devices: 72 us -> 82.3 us
  starting transfers between devices: 57.2 us -> 48.9 us
    ppermute x34 -> x28, waiting for transfers between devices: 72 us -> 82.3 us  [swap(): lax.ppermute(x, axis, [(i, i ^ mask) for i in range(lax.axis_size(axis))])]
    ppermute x34 -> x28, starting transfers between devices: 53.3 us -> 44.9 us  [swap(): lax.ppermute(x, axis, [(i, i ^ mask) for i in range(lax.axis_size(axis))])]
  transfers between devices with their start and end apart: 38 -> 32, of which waited for: 14 -> 15; matrix products, arithmetic and copies ran while one was open for 1% -> 1% of each run, Pallas kernels for 21% -> 20%
where the time goes in v2:
time: 180 us
  waiting for transfers between devices  82.3 us (46%)
  starting transfers between devices  48.9 us (27%)
  Pallas kernels  42.4 us (24%)
  local copies, waits for them, and re-layouts  2.31 us (1%)
  other arithmetic  2.04 us (1%)
  between operations  1.83 us (1%)
    ppermute x28, waiting for transfers between devices, swap(): lax.ppermute(x, axis, [(i, i ^ mask) for i in range(lax.axis_size(axis))])  82.3 us
    ppermute x28, starting transfers between devices, swap(): lax.ppermute(x, axis, [(i, i ^ mask) for i in range(lax.axis_size(axis))])  44.9 us
    pallas_call x8, Pallas kernels, call(): pl.pallas_call(kernel, grid_spec=pltpu.PrefetchScalarGridSpec(num_scalar_...  42.4 us
  transfers between devices with their start and end apart: 32, of which 15 were waited for; matrix products, arithmetic and copies ran while one was open for 1% of the time, Pallas kernels for 20%

profile of v2, /device:TPU:0, one launch (start us, length us, event | category | flops | bytes accessed | tf_op | source)
XLA Modules:
  0.0 179.8 jit_solution(8307789535424869868)
XLA Ops:
  0.6 3.1 %collective-permute-start.3 = (bf16[256,1024]{1,0:T(8,128)(2,1)}, bf16[256,1024]{1,0:T(8,128)(2,1)S(1)}, u32[]{:S(2)}, u32[]{:S(2)}) collective-permute-start(bf16[256,1024]{1,0:T(8,128)(2,1)} %bitcast.85), channel_id=1, source_target_pairs={{0,1},{1,0},{2,3},{3,2},{4,5},{5,4},{6,7},{7,6},{8,9},{9,8},{10,11... | collective-permute-start | bytes 1572872 | tf_op jit(solution)/shard_map/ppermute | solution.py:312
  3.7 0.7 collective-permute-start.5
  4.4 11.4 %collective-permute-done.3.refs_5_ = bf16[256,1024]{1,0:T(8,128)(2,1)S(1)} collective-permute-done((bf16[256,1024]{1,0:T(8,128)(2,1)}, bf16[256,1024]{1,0:T(8,128)(2,1)S(1)}, u32[]{:S(2)}, u32[]{:S(2)}) %collective-permute-start.3) | collective-permute-done | bytes 524320 | tf_op jit(solution)/shard_map/ppermute | solution.py:312
  15.9 0.7 collective-permute-start.4
  16.6 0.0 copy-start
  16.6 2.2 %copy-done = bf16[1,256,8192]{2,1,0:T(8,128)(2,1)S(1)} copy-done((bf16[1,256,8192]{2,1,0:T(8,128)(2,1)S(1)}, bf16[1,256,8192]{2,1,0:T(8,128)(2,1)}, u32[]{:S(2)}) %copy-start) | copy-done | bytes 4194328
  18.8 5.0 %shard_map.128 = (bf16[8,64,256]{2,1,0:T(8,128)(2,1)S(1)}, bf16[8,64,256]{2,1,0:T(8,128)(2,1)S(1)}, bf16[8,64,256]{2,1,0:T(8,128)(2,1)S(1)}, bf16[8,64,256]{2,1,...) custom-call(s32[12]{0:T(128)S(1)} %compare_select_fusion.table_ref, ...), custom_call_target="tpu_custom_call" | custom-call | bytes 4194304 | tf_op jit(solution)/shard_map/pallas_call | solution.py:44
  23.8 3.8 %collective-permute-start.10 = (bf16[8,64,256]{2,1,0:T(8,128)(2,1)S(1)}, bf16[8,64,256]{2,1,0:T(8,128)(2,1)S(1)}, u32[]{:S(2)}, u32[]{:S(2)}) collective-permute-start(bf16[8,64,256]{2,1,0:T(8,128)(2,1)S(1)} %get-tuple-element.42), channel_id=1, source_target_pairs={{0,3},{1,2},{2,1},{3,0},{4,7},{5,6},{6,5},{7,4},{8,11},{9,10},{10,... | collective-permute-start | bytes 786440 | tf_op jit(solution)/shard_map/ppermute | solution.py:312
  27.7 4.5 %shard_map.129 = (bf16[8,144,256]{2,1,0:T(8,128)(2,1)S(1)}, bf16[8,144,256]{2,1,0:T(8,128)(2,1)S(1)}, bf16[8,144,256]{2,1,0:T(8,128)(2,1)S(1)}, bf16[8,144,256]{2,1,0:T(8,128)(2,1)S(1)}) custom-call(s32[12]{0:T(128)S(1)} %compare_select_fusion.table_ref, bf16[256,8192]{1,0:T(8,128)(2,1)S(1)} %bitcast.84), custom_call_target="tpu_custom_call" | custom-call | bytes 8388608 | tf_op jit(solution)/shard_map/pallas_call | solution.py:44
  32.1 1.3 collective-permute-start.11
  33.4 1.1 collective-permute-start.12
  34.5 2.6 %collective-permute-start.13 = (bf16[8,144,256]{2,1,0:T(8,128)(2,1)S(1)}, bf16[8,144,256]{2,1,0:T(8,128)(2,1)S(1)}, u32[]{:S(2)}, u32[]{:S(2)}) collective-permute-start(bf16[8,144,256]{2,1,0:T(8,128)(2,1)S(1)} %get-tuple-element.46), channel_id=1, source_target_pairs={{0,3},{1,2},{2,1},{3,0},{4,7},{5,6},{6,5},{7,4},{8,11},{9,10},{10,... | collective-permute-start | bytes 1769480 | tf_op jit(solution)/shard_map/ppermute | solution.py:312
  37.2 1.3 collective-permute-start.6
  38.5 1.3 collective-permute-start.7
  39.8 13.3 %collective-permute-done.11.refs_1_ = bf16[8,144,256]{2,1,0:T(8,128)(2,1)S(1)} collective-permute-done((bf16[8,144,256]{2,1,0:T(8,128)(2,1)S(1)}, bf16[8,144,256]{2,1,0:T(8,128)(2,1)S(1)}, u32[]{:S(2)}, u32[]{:S(2)}) %collective-permute-start.11) | collective-permute-done | bytes 589856 | tf_op jit(solution)/shard_map/ppermute | solution.py:312
  53.0 32.7 %collective-permute-done.12.refs_2_ = bf16[8,144,256]{2,1,0:T(8,128)(2,1)S(1)} collective-permute-done((bf16[8,144,256]{2,1,0:T(8,128)(2,1)S(1)}, bf16[8,144,256]{2,1,0:T(8,128)(2,1)S(1)}, u32[]{:S(2)}, u32[]{:S(2)}) %collective-permute-start.12) | collective-permute-done | bytes 589856 | tf_op jit(solution)/shard_map/ppermute | solution.py:312
  86.4 15.3 %collective-permute-start = (bf16[8,48,256]{2,1,0:T(8,128)(2,1)S(1)}, bf16[8,48,256]{2,1,0:T(8,128)(2,1)S(1)}, u32[]{:S(2)}, u32[]{:S(2)}) collective-permute-start(bf16[8,48,256]{2,1,0:T(8,128)(2,1)S(1)} %get-tuple-element.36), channel_id=1, source_target_pairs={{0,1},{1,0},{2,3},{3,2},{4,5},{5,4},{6,7},{7,6},{8,9},{9,8},{10,11... | collective-permute-start | bytes 589832 | tf_op jit(solution)/shard_map/ppermute | solution.py:312
  101.8 1.0 collective-permute-start.1
  102.8 1.5 collective-permute-start.2
  104.3 11.7 %shard_map.130 = (f32[8,256,1024]{2,1,0:T(8,128)}, bf16[8,256,1024]{2,1,0:T(8,128)(2,1)}, bf16[8,256,1024]{2,1,0:T(8,128)(2,1)}, bf16[4,144,512]{2,1,0:T(8,128)(2,1)S(1)}, bf16[4,144,512]{2,1,0:T(8,128)(2,1)S(1)}) custom-call(s32[8]{0:T(128)S(1)} %copy-done.2, s32[1]{0:T(128)S(6)} %copy.36.step_ref, s32[12]{0:T(128)S(1)} %compare_select_fusion.table_ref, ...), custom_call_target="tpu_custom_call" | custom-call | flops 2415919104 | bytes 21233664 | tf_op jit(solution)/shard_map/pallas_call | solution.py:44
  116.0 8.0 %shard_map.131 = (f32[8,256,1024]{2,1,0:T(8,128)}, bf16[8,256,1024]{2,1,0:T(8,128)(2,1)}, bf16[8,256,1024]{2,1,0:T(8,128)(2,1)}, bf16[4,64,512]{2,1,0:T(8,128)(2,1)S(1)}, bf16[4,64,512]{2,1,0:T(8,128)(2,1)S(1)}) custom-call(s32[8]{0:T(128)S(1)} %copy-done.2, s32[1]{0:T(128)S(6)} %copy.36.step_ref, ...), custom_call_target="tpu_custom_call", output_to_operand_aliasing={{0}: (16, {}), {1}: (17, {}), {2}: (18, {})} | custom-call | flops 1073741824 | bytes 9437184 | tf_op jit(solution)/shard_map/pallas_call | solution.py:44
  124.1 4.7 %shard_map.132 = (f32[8,256,1024]{2,1,0:T(8,128)}, bf16[8,256,1024]{2,1,0:T(8,128)(2,1)}, bf16[8,256,1024]{2,1,0:T(8,128)(2,1)}, bf16[4,48,512]{2,1,0:T(8,128)(2,1)S(1)}, bf16[4,48,512]{2,1,0:T(8,128)(2,1)S(1)}) custom-call(s32[8]{0:T(128)S(1)} %copy-done.2, s32[1]{0:T(128)S(6)} %copy.36.step_ref, ...), custom_call_target="tpu_custom_call", output_to_operand_aliasing={{0}: (16, {}), {1}: (17, {}), {2}: (18, {})} | custom-call | flops 402653184 | bytes 3932160 | tf_op jit(solution)/shard_map/pallas_call | solution.py:44
  128.8 0.1 collective-permute-start.14
  128.9 0.5 collective-permute-start.16
  129.4 0.1 collective-permute-start.15
  129.5 0.9 collective-permute-done.14
  130.3 0.1 convert_add_fusion.2
  130.4 1.1 collective-permute-done.15
  131.5 0.1 convert_add_fusion.1
  131.6 0.2 convert_add_fusion
  131.9 1.6 collective-permute-start.17
  133.5 1.5 collective-permute-start.18
  135.0 0.5 collective-permute-start.19
  135.5 3.2 %collective-permute-done.17 = bf16[144,512]{1,0:T(8,128)(2,1)S(1)} collective-permute-done((bf16[144,512]{1,0:T(8,128)(2,1)S(1)}, bf16[144,512]{1,0:T(8,128)(2,1)S(1)}, u32[]{:S(2)}, u32[]{:S(2)}) %collective-permute-start.17) | collective-permute-done | bytes 147488 | tf_op jit(solution)/shard_map/ppermute | solution.py:312
  138.7 3.6 %collective-permute-done.18 = bf16[144,512]{1,0:T(8,128)(2,1)S(1)} collective-permute-done((bf16[144,512]{1,0:T(8,128)(2,1)S(1)}, bf16[144,512]{1,0:T(8,128)(2,1)S(1)}, u32[]{:S(2)}, u32[]{:S(2)}) %collective-permute-start.18) | collective-permute-done | bytes 147488 | tf_op jit(solution)/shard_map/ppermute | solution.py:312
  142.3 0.1 multiply_add_fusion
  142.5 0.1 fusion.23
  142.6 0.1 pad_maximum_fusion.6
  142.6 1.3 collective-permute-start.20
  143.9 0.8 collective-permute-start.21
  144.8 1.4 collective-permute-start.22
  146.2 4.6 %collective-permute-done.20 = bf16[208,512]{1,0:T(8,128)(2,1)S(1)} collective-permute-done((bf16[208,512]{1,0:T(8,128)(2,1)S(1)}, bf16[208,512]{1,0:T(8,128)(2,1)S(1)}, u32[]{:S(2)}, u32[]{:S(2)}) %collective-permute-start.20) | collective-permute-done | bytes 213024 | tf_op jit(solution)/shard_map/ppermute | solution.py:312
  150.8 3.9 %collective-permute-done.21 = bf16[208,512]{1,0:T(8,128)(2,1)S(1)} collective-permute-done((bf16[208,512]{1,0:T(8,128)(2,1)S(1)}, bf16[208,512]{1,0:T(8,128)(2,1)S(1)}, u32[]{:S(2)}, u32[]{:S(2)}) %collective-permute-start.21) | collective-permute-done | bytes 213024 | tf_op jit(solution)/shard_map/ppermute | solution.py:312
  154.7 0.1 multiply_add_fusion.1
  154.9 0.6 collective-permute-start.23
  155.5 1.4 collective-permute-start.24
  157.0 1.5 collective-permute-start.25
  158.5 0.1 pad_maximum_fusion.refs_0_
  158.6 0.1 collective-permute-start.30
  158.7 1.1 collective-permute-done.23
  159.7 1.2 collective-permute-done.24
  160.9 2.1 %collective-permute-done.25 = bf16[112,512]{1,0:T(8,128)(2,1)S(1)} collective-permute-done((bf16[112,512]{1,0:T(8,128)(2,1)S(1)}, bf16[112,512]{1,0:T(8,128)(2,1)S(1)}, u32[]{:S(2)}, u32[]{:S(2)}) %collective-permute-start.25) | collective-permute-done | bytes 114720 | tf_op jit(solution)/shard_map/ppermute | solution.py:312
  163.1 0.3 collective-permute-start.26
  163.4 1.5 collective-permute-start.27
  164.9 1.8 collective-permute-start.28
  166.7 0.1 collective-permute-start.31
  166.8 0.4 collective-permute-done.26
  167.3 0.2 collective-permute-done.27
  167.5 2.4 %collective-permute-done.28 = bf16[48,512]{1,0:T(8,128)(2,1)S(1)} collective-permute-done((bf16[48,512]{1,0:T(8,128)(2,1)S(1)}, bf16[48,512]{1,0:T(8,128)(2,1)S(1)}, u32[]{:S(2)}, u32[]{:S(2)}) %collective-permute-start.28) | collective-permute-done | bytes 49184 | tf_op jit(solution)/shard_map/ppermute | solution.py:312
  169.9 0.1 collective-permute-start.29
  170.0 4.7 %shard_map.133 = (f32[8,256,1024]{2,1,0:T(8,128)}, bf16[8,256,1024]{2,1,0:T(8,128)(2,1)}, bf16[8,256,1024]{2,1,0:T(8,128)(2,1)}) custom-call(s32[8]{0:T(128)S(1)} %copy-done.2, s32[1]{0:T(128)S(6)} %copy.36.step_ref, s32[12]{0:T(128)S(1)} %compare_select_fusion.table_ref, ...), custom_call_target="tpu_custom_call", output_to_operand_aliasing={{0}: (16, {}), {1}: (17, {}), {2}: (18, {})} | custom-call | flops 402653184 | bytes 3932160 | tf_op jit(solution)/shard_map/pallas_call | solution.py:44
  174.7 1.0 pad_maximum_fusion.1
  175.7 2.4 %shard_map.134.refs_2_ = f32[8,256,1024]{2,1,0:T(8,128)} custom-call(s32[8]{0:T(128)S(1)} %copy-done.2, s32[1]{0:T(128)S(6)} %copy.36.step_ref, s32[12]{0:T(128)S(1)} %compare_select_fusion.table_ref, bf16[4,144,512]{2,1,0:T(8,128)(2,1)S(1)} %pad_maximum_fusion.refs_0_, ...), custom_call_target="tpu_custom_call", output_to_operand_aliasing={{}: (7, {})} | custom-call | bytes 6815744 | tf_op jit(solution)/shard_map/pallas_call | solution.py:44
  178.1 1.5 shard_map.135
  (43 shorter events, 0.4 us)
Async XLA Ops:
  0.6 15.3 %collective-permute-start.3 = (bf16[256,1024]{1,0:T(8,128)(2,1)}, bf16[256,1024]{1,0:T(8,128)(2,1)S(1)}, u32[]{:S(2)}, u32[]{:S(2)}) collective-permute-start(bf16[256,1024]{1,0:T(8,128)(2,1)} %bitcast.85), channel_id=1, source_target_pairs={{0,1},{1,0},{2,3},{3,2},{4,5},{5,4},{6,7},{7,6},{8,9},{9,8},{10,11... | collective-permute-start | bytes 1572872 | tf_op jit(solution)/shard_map/ppermute | solution.py:312
  3.7 33.4 %collective-permute-start.5 = (bf16[256,1024]{1,0:T(8,128)(2,1)}, bf16[256,1024]{1,0:T(8,128)(2,1)S(1)}, u32[]{:S(2)}, u32[]{:S(2)}) collective-permute-start(bf16[256,1024]{1,0:T(8,128)(2,1)} %bitcast.86), channel_id=1, source_target_pairs={{1,2},{2,1},{5,6},{6,5},{9,10},{10,9},{13,14},{14,13},{17,18},{18,... | collective-permute-start | bytes 1572872 | tf_op jit(solution)/shard_map/ppermute | solution.py:318
  15.9 22.6 %collective-permute-start.4 = (bf16[256,1024]{1,0:T(8,128)(2,1)S(1)}, bf16[256,1024]{1,0:T(8,128)(2,1)S(1)}, u32[]{:S(2)}, u32[]{:S(2)}) collective-permute-start(bf16[256,1024]{1,0:T(8,128)(2,1)S(1)} %collective-permute-done.3.refs_5_), channel_id=1, source_target_pairs={{1,2},{2,1},{5,6},{6,5},{9,10},{10,9},{13,14},{14,13},{17,18},{18,... | collective-permute-start | bytes 1572872 | tf_op jit(solution)/shard_map/ppermute | solution.py:319
  16.6 2.2 %copy-start = (bf16[1,256,8192]{2,1,0:T(8,128)(2,1)S(1)}, bf16[1,256,8192]{2,1,0:T(8,128)(2,1)}, u32[]{:S(2)}) copy-start(bf16[1,256,8192]{2,1,0:T(8,128)(2,1)} %param.9) | copy-start | bytes 12582916
  18.8 85.5 %copy-start.1 = (bf16[1,256,1024]{2,1,0:T(8,128)(2,1)S(1)}, bf16[1,256,1024]{2,1,0:T(8,128)(2,1)}, u32[]{:S(2)}) copy-start(bf16[1,256,1024]{2,1,0:T(8,128)(2,1)} %param.10) | copy-start | bytes 1572868
  18.8 85.5 %copy-start.2 = (s32[8]{0:T(128)S(1)}, s32[8]{0:T(128)}, u32[]{:S(2)}) copy-start(s32[8]{0:T(128)} %heads_ref.11) | copy-start | bytes 100
  23.8 10.7 %collective-permute-start.10 = (bf16[8,64,256]{2,1,0:T(8,128)(2,1)S(1)}, bf16[8,64,256]{2,1,0:T(8,128)(2,1)S(1)}, u32[]{:S(2)}, u32[]{:S(2)}) collective-permute-start(bf16[8,64,256]{2,1,0:T(8,128)(2,1)S(1)} %get-tuple-element.42), channel_id=1, source_target_pairs={{0,3},{1,2},{2,1},{3,0},{4,7},{5,6},{6,5},{7,4},{8,11},{9,10},{10,... | collective-permute-start | bytes 786440 | tf_op jit(solution)/shard_map/ppermute | solution.py:312
  32.1 20.9 %collective-permute-start.11 = (bf16[8,144,256]{2,1,0:T(8,128)(2,1)S(1)}, bf16[8,144,256]{2,1,0:T(8,128)(2,1)S(1)}, u32[]{:S(2)}, u32[]{:S(2)}) collective-permute-start(bf16[8,144,256]{2,1,0:T(8,128)(2,1)S(1)} %get-tuple-element.44), channel_id=1, source_target_pairs={{0,1},{1,0},{2,3},{3,2},{4,5},{5,4},{6,7},{7,6},{8,9},{9,8},{10,11... | collective-permute-start | bytes 1769480 | tf_op jit(solution)/shard_map/ppermute | solution.py:312
  33.4 52.3 %collective-permute-start.12 = (bf16[8,144,256]{2,1,0:T(8,128)(2,1)S(1)}, bf16[8,144,256]{2,1,0:T(8,128)(2,1)S(1)}, u32[]{:S(2)}, u32[]{:S(2)}) collective-permute-start(bf16[8,144,256]{2,1,0:T(8,128)(2,1)S(1)} %get-tuple-element.45), channel_id=1, source_target_pairs={{0,2},{1,3},{2,0},{3,1},{4,6},{5,7},{6,4},{7,5},{8,10},{9,11},{10,... | collective-permute-start | bytes 1769480 | tf_op jit(solution)/shard_map/ppermute | solution.py:312
  34.5 51.9 %collective-permute-start.13 = (bf16[8,144,256]{2,1,0:T(8,128)(2,1)S(1)}, bf16[8,144,256]{2,1,0:T(8,128)(2,1)S(1)}, u32[]{:S(2)}, u32[]{:S(2)}) collective-permute-start(bf16[8,144,256]{2,1,0:T(8,128)(2,1)S(1)} %get-tuple-element.46), channel_id=1, source_target_pairs={{0,3},{1,2},{2,1},{3,0},{4,7},{5,6},{6,5},{7,4},{8,11},{9,10},{10,... | collective-permute-start | bytes 1769480 | tf_op jit(solution)/shard_map/ppermute | solution.py:312
  37.2 64.6 %collective-permute-start.6 = (bf16[256,1024]{1,0:T(8,128)(2,1)S(1)}, bf16[256,1024]{1,0:T(8,128)(2,1)S(1)}, u32[]{:S(2)}, u32[]{:S(2)}) collective-permute-start(bf16[256,1024]{1,0:T(8,128)(2,1)S(1)} %collective-permute-done.5.refs_8_), channel_id=1, source_target_pairs={{1,0},{2,3},{5,4},{6,7},{9,8},{10,11},{13,12},{14,15},{17,16},{18,... | collective-permute-start | bytes 1572872 | tf_op jit(solution)/shard_map/ppermute | solution.py:320
  38.5 64.3 %collective-permute-start.7 = (bf16[256,1024]{1,0:T(8,128)(2,1)S(1)}, bf16[256,1024]{1,0:T(8,128)(2,1)S(1)}, u32[]{:S(2)}, u32[]{:S(2)}) collective-permute-start(bf16[256,1024]{1,0:T(8,128)(2,1)S(1)} %collective-permute-done.4.refs_6_), channel_id=1, source_target_pairs={{1,0},{2,3},{5,4},{6,7},{9,8},{10,11},{13,12},{14,15},{17,16},{18,... | collective-permute-start | bytes 1572872 | tf_op jit(solution)/shard_map/ppermute | solution.py:321
  53.0 62.9 %collective-permute-start.8 = (bf16[8,64,256]{2,1,0:T(8,128)(2,1)S(1)}, bf16[8,64,256]{2,1,0:T(8,128)(2,1)S(1)}, u32[]{:S(2)}, u32[]{:S(2)}) collective-permute-start(bf16[8,64,256]{2,1,0:T(8,128)(2,1)S(1)} %get-tuple-element.40), channel_id=1, source_target_pairs={{0,1},{1,0},{2,3},{3,2},{4,5},{5,4},{6,7},{7,6},{8,9},{9,8},{10,11... | collective-permute-start | bytes 786440 | tf_op jit(solution)/shard_map/ppermute | solution.py:312
  85.7 30.3 %collective-permute-start.9 = (bf16[8,64,256]{2,1,0:T(8,128)(2,1)S(1)}, bf16[8,64,256]{2,1,0:T(8,128)(2,1)S(1)}, u32[]{:S(2)}, u32[]{:S(2)}) collective-permute-start(bf16[8,64,256]{2,1,0:T(8,128)(2,1)S(1)} %get-tuple-element.41), channel_id=1, source_target_pairs={{0,2},{1,3},{2,0},{3,1},{4,6},{5,7},{6,4},{7,5},{8,10},{9,11},{10,... | collective-permute-start | bytes 786440 | tf_op jit(solution)/shard_map/ppermute | solution.py:312
  86.4 37.7 %collective-permute-start = (bf16[8,48,256]{2,1,0:T(8,128)(2,1)S(1)}, bf16[8,48,256]{2,1,0:T(8,128)(2,1)S(1)}, u32[]{:S(2)}, u32[]{:S(2)}) collective-permute-start(bf16[8,48,256]{2,1,0:T(8,128)(2,1)S(1)} %get-tuple-element.36), channel_id=1, source_target_pairs={{0,1},{1,0},{2,3},{3,2},{4,5},{5,4},{6,7},{7,6},{8,9},{9,8},{10,11... | collective-permute-start | bytes 589832 | tf_op jit(solution)/shard_map/ppermute | solution.py:312
  101.8 22.3 %collective-permute-start.1 = (bf16[8,48,256]{2,1,0:T(8,128)(2,1)S(1)}, bf16[8,48,256]{2,1,0:T(8,128)(2,1)S(1)}, u32[]{:S(2)}, u32[]{:S(2)}) collective-permute-start(bf16[8,48,256]{2,1,0:T(8,128)(2,1)S(1)} %get-tuple-element.37), channel_id=1, source_target_pairs={{0,2},{1,3},{2,0},{3,1},{4,6},{5,7},{6,4},{7,5},{8,10},{9,11},{10,... | collective-permute-start | bytes 589832 | tf_op jit(solution)/shard_map/ppermute | solution.py:312
  102.8 21.3 %collective-permute-start.2 = (bf16[8,48,256]{2,1,0:T(8,128)(2,1)S(1)}, bf16[8,48,256]{2,1,0:T(8,128)(2,1)S(1)}, u32[]{:S(2)}, u32[]{:S(2)}) collective-permute-start(bf16[8,48,256]{2,1,0:T(8,128)(2,1)S(1)} %get-tuple-element.38), channel_id=1, source_target_pairs={{0,3},{1,2},{2,1},{3,0},{4,7},{5,6},{6,5},{7,4},{8,11},{9,10},{10,... | collective-permute-start | bytes 589832 | tf_op jit(solution)/shard_map/ppermute | solution.py:312
  128.8 13.5 %copy-start.3 = (f32[256,512]{1,0:T(8,128)S(1)}, f32[256,512]{1,0:T(8,128)}, u32[]{:S(2)}) copy-start(f32[256,512]{1,0:T(8,128)} %param.15) | copy-start | bytes 1572868
  128.8 13.5 %copy-start.4 = (f32[256,512]{1,0:T(8,128)S(1)}, f32[256,512]{1,0:T(8,128)}, u32[]{:S(2)}) copy-start(f32[256,512]{1,0:T(8,128)} %param.14) | copy-start | bytes 1572868
  128.8 1.5 collective-permute-start.14
  128.9 2.8 %collective-permute-start.16 = (bf16[4,144,512]{2,1,0:T(8,128)(2,1)S(1)}, bf16[4,144,512]{2,1,0:T(8,128)(2,1)S(1)}, u32[]{:S(2)}, u32[]{:S(2)}) collective-permute-start(bf16[4,144,512]{2,1,0:T(8,128)(2,1)S(1)} %get-tuple-element.58), channel_id=1, source_target_pairs={{0,4},{4,0},{8,12},{12,8},{16,20},{20,16},{24,28},{28,24},{1,5},{5... | collective-permute-start | bytes 1769480 | tf_op jit(solution)/shard_map/ppermute | solution.py:312
  129.4 2.1 %collective-permute-start.15 = (bf16[4,64,512]{2,1,0:T(8,128)(2,1)S(1)}, bf16[4,64,512]{2,1,0:T(8,128)(2,1)S(1)}, u32[]{:S(2)}, u32[]{:S(2)}) collective-permute-start(bf16[4,64,512]{2,1,0:T(8,128)(2,1)S(1)} %get-tuple-element.56), channel_id=1, source_target_pairs={{0,4},{4,0},{8,12},{12,8},{16,20},{20,16},{24,28},{28,24},{1,5},{5... | collective-permute-start | bytes 786440 | tf_op jit(solution)/shard_map/ppermute | solution.py:312
  131.9 6.8 %collective-permute-start.17 = (bf16[144,512]{1,0:T(8,128)(2,1)S(1)}, bf16[144,512]{1,0:T(8,128)(2,1)S(1)}, u32[]{:S(2)}, u32[]{:S(2)}) collective-permute-start(bf16[144,512]{1,0:T(8,128)(2,1)S(1)} %get-tuple-element.79), channel_id=1, source_target_pairs={{0,8},{4,12},{8,0},{12,4},{16,24},{20,28},{24,16},{28,20},{1,9},{5... | collective-permute-start | bytes 442376 | tf_op jit(solution)/shard_map/ppermute | solution.py:312
  133.5 8.9 %collective-permute-start.18 = (bf16[144,512]{1,0:T(8,128)(2,1)S(1)}, bf16[144,512]{1,0:T(8,128)(2,1)S(1)}, u32[]{:S(2)}, u32[]{:S(2)}) collective-permute-start(bf16[144,512]{1,0:T(8,128)(2,1)S(1)} %get-tuple-element.81), channel_id=1, source_target_pairs={{0,16},{4,20},{8,24},{12,28},{16,0},{20,4},{24,8},{28,12},{1,17},{... | collective-permute-start | bytes 442376 | tf_op jit(solution)/shard_map/ppermute | solution.py:312
  135.0 7.4 %collective-permute-start.19 = (bf16[144,512]{1,0:T(8,128)(2,1)S(1)}, bf16[144,512]{1,0:T(8,128)(2,1)S(1)}, u32[]{:S(2)}, u32[]{:S(2)}) collective-permute-start(bf16[144,512]{1,0:T(8,128)(2,1)S(1)} %get-tuple-element.80), channel_id=1, source_target_pairs={{0,24},{4,28},{8,16},{12,20},{16,8},{20,12},{24,0},{28,4},{1,25},{... | collective-permute-start | bytes 442376 | tf_op jit(solution)/shard_map/ppermute | solution.py:312
  142.6 8.2 %collective-permute-start.20 = (bf16[208,512]{1,0:T(8,128)(2,1)S(1)}, bf16[208,512]{1,0:T(8,128)(2,1)S(1)}, u32[]{:S(2)}, u32[]{:S(2)}) collective-permute-start(bf16[208,512]{1,0:T(8,128)(2,1)S(1)} %get-tuple-element.92), channel_id=1, source_target_pairs={{0,8},{4,12},{8,0},{12,4},{16,24},{20,28},{24,16},{28,20},{1,9},{5... | collective-permute-start | bytes 638984 | tf_op jit(solution)/shard_map/ppermute | solution.py:312
  143.9 10.8 %collective-permute-start.21 = (bf16[208,512]{1,0:T(8,128)(2,1)S(1)}, bf16[208,512]{1,0:T(8,128)(2,1)S(1)}, u32[]{:S(2)}, u32[]{:S(2)}) collective-permute-start(bf16[208,512]{1,0:T(8,128)(2,1)S(1)} %get-tuple-element.93), channel_id=1, source_target_pairs={{0,16},{4,20},{8,24},{12,28},{16,0},{20,4},{24,8},{28,12},{1,17},{... | collective-permute-start | bytes 638984 | tf_op jit(solution)/shard_map/ppermute | solution.py:312
  144.8 10.0 %collective-permute-start.22 = (bf16[208,512]{1,0:T(8,128)(2,1)S(1)}, bf16[208,512]{1,0:T(8,128)(2,1)S(1)}, u32[]{:S(2)}, u32[]{:S(2)}) collective-permute-start(bf16[208,512]{1,0:T(8,128)(2,1)S(1)} %get-tuple-element.94), channel_id=1, source_target_pairs={{0,24},{4,28},{8,16},{12,20},{16,8},{20,12},{24,0},{28,4},{1,25},{... | collective-permute-start | bytes 638984 | tf_op jit(solution)/shard_map/ppermute | solution.py:312
  154.9 4.9 %collective-permute-start.23 = (bf16[112,512]{1,0:T(8,128)(2,1)S(1)}, bf16[112,512]{1,0:T(8,128)(2,1)S(1)}, u32[]{:S(2)}, u32[]{:S(2)}) collective-permute-start(bf16[112,512]{1,0:T(8,128)(2,1)S(1)} %get-tuple-element.95), channel_id=1, source_target_pairs={{0,8},{4,12},{8,0},{12,4},{16,24},{20,28},{24,16},{28,20},{1,9},{5... | collective-permute-start | bytes 344072 | tf_op jit(solution)/shard_map/ppermute | solution.py:312
  155.5 5.4 %collective-permute-start.24 = (bf16[112,512]{1,0:T(8,128)(2,1)S(1)}, bf16[112,512]{1,0:T(8,128)(2,1)S(1)}, u32[]{:S(2)}, u32[]{:S(2)}) collective-permute-start(bf16[112,512]{1,0:T(8,128)(2,1)S(1)} %get-tuple-element.96), channel_id=1, source_target_pairs={{0,16},{4,20},{8,24},{12,28},{16,0},{20,4},{24,8},{28,12},{1,17},{... | collective-permute-start | bytes 344072 | tf_op jit(solution)/shard_map/ppermute | solution.py:312
  157.0 6.0 %collective-permute-start.25 = (bf16[112,512]{1,0:T(8,128)(2,1)S(1)}, bf16[112,512]{1,0:T(8,128)(2,1)S(1)}, u32[]{:S(2)}, u32[]{:S(2)}) collective-permute-start(bf16[112,512]{1,0:T(8,128)(2,1)S(1)} %get-tuple-element.97), channel_id=1, source_target_pairs={{0,24},{4,28},{8,16},{12,20},{16,8},{20,12},{24,0},{28,4},{1,25},{... | collective-permute-start | bytes 344072 | tf_op jit(solution)/shard_map/ppermute | solution.py:312
  158.6 17.1 %collective-permute-start.30 = (bf16[4,144,512]{2,1,0:T(8,128)(2,1)S(1)}, bf16[4,144,512]{2,1,0:T(8,128)(2,1)S(1)}, u32[]{:S(2)}, u32[]{:S(2)}) collective-permute-start(bf16[4,144,512]{2,1,0:T(8,128)(2,1)S(1)} %pad_maximum_fusion.refs_0_), channel_id=1, source_target_pairs={{0,4},{4,0},{8,12},{12,8},{16,20},{20,16},{24,28},{28,24},{1,5},{5... | collective-permute-start | bytes 1769480 | tf_op jit(solution)/shard_map/ppermute | solution.py:312
  163.1 4.2 %collective-permute-start.26 = (bf16[48,512]{1,0:T(8,128)(2,1)S(1)}, bf16[48,512]{1,0:T(8,128)(2,1)S(1)}, u32[]{:S(2)}, u32[]{:S(2)}) collective-permute-start(bf16[48,512]{1,0:T(8,128)(2,1)S(1)} %get-tuple-element.71), channel_id=1, source_target_pairs={{0,8},{4,12},{8,0},{12,4},{16,24},{20,28},{24,16},{28,20},{1,9},{5... | collective-permute-start | bytes 147464 | tf_op jit(solution)/shard_map/ppermute | solution.py:312
  163.4 4.1 %collective-permute-start.27 = (bf16[48,512]{1,0:T(8,128)(2,1)S(1)}, bf16[48,512]{1,0:T(8,128)(2,1)S(1)}, u32[]{:S(2)}, u32[]{:S(2)}) collective-permute-start(bf16[48,512]{1,0:T(8,128)(2,1)S(1)} %get-tuple-element.71), channel_id=1, source_target_pairs={{0,16},{4,20},{8,24},{12,28},{16,0},{20,4},{24,8},{28,12},{1,17},{... | collective-permute-start | bytes 147464 | tf_op jit(solution)/shard_map/ppermute | solution.py:312
  164.9 5.0 %collective-permute-start.28 = (bf16[48,512]{1,0:T(8,128)(2,1)S(1)}, bf16[48,512]{1,0:T(8,128)(2,1)S(1)}, u32[]{:S(2)}, u32[]{:S(2)}) collective-permute-start(bf16[48,512]{1,0:T(8,128)(2,1)S(1)} %get-tuple-element.71), channel_id=1, source_target_pairs={{0,24},{4,28},{8,16},{12,20},{16,8},{20,12},{24,0},{28,4},{1,25},{... | collective-permute-start | bytes 147464 | tf_op jit(solution)/shard_map/ppermute | solution.py:312
  166.7 9.0 %collective-permute-start.31 = (bf16[4,64,512]{2,1,0:T(8,128)(2,1)S(1)}, bf16[4,64,512]{2,1,0:T(8,128)(2,1)S(1)}, u32[]{:S(2)}, u32[]{:S(2)}) collective-permute-start(bf16[4,64,512]{2,1,0:T(8,128)(2,1)S(1)} %pad_maximum_fusion.3.refs_2_), channel_id=1, source_target_pairs={{0,4},{4,0},{8,12},{12,8},{16,20},{20,16},{24,28},{28,24},{1,5},{5... | collective-permute-start | bytes 786440 | tf_op jit(solution)/shard_map/ppermute | solution.py:312
  169.9 8.2 %collective-permute-start.29 = (bf16[4,48,512]{2,1,0:T(8,128)(2,1)S(1)}, bf16[4,48,512]{2,1,0:T(8,128)(2,1)S(1)}, u32[]{:S(2)}, u32[]{:S(2)}) collective-permute-start(bf16[4,48,512]{2,1,0:T(8,128)(2,1)S(1)} %pad_maximum_fusion.7.refs_0_), channel_id=1, source_target_pairs={{0,4},{4,0},{8,12},{12,8},{16,20},{20,16},{24,28},{28,24},{1,5},{5... | collective-permute-start | bytes 589832 | tf_op jit(solution)/shard_map/ppermute | solution.py:312
